TPU v7x, 512 devices: a whole 4x4x16 slice. The times are simulated.
512 devices in a mesh: rows: 128 (over z, y, core), edges: 4 (over x).
Axes of the slice: x: 4, y: 4, z: 16, core: 2. Of those that a mesh axis runs over, the one named last changes fastest.
Arguments:
- features: bfloat16 [655360, 256], P(('rows', 'edges')), may hold values from -6 to 6
- edge_src: int32 [655360], P(('rows', 'edges')), may hold values from 0 to 16383, as said below
- edge_dst: int32 [655360], P(('rows', 'edges')), may hold values from 0 to 16383, as said below
- edge_cell: int32 [655360], P(('rows', 'edges')), may hold values from 0 to 2
- cell_bias: bfloat16 [3, 512], replicated, may hold values from -4 to 4
- w_in: bfloat16 [256, 512], replicated, may hold values from -0.375 to 0.375
- w_out: bfloat16 [256, 256], replicated, may hold values from -0.0068359375 to 0.0068359375
- vectors: float32 [128, 262144], P('edges', 'rows'), may hold values from -6 to 6
- cheb_coef: float32 [5], replicated, may hold values from 0.5 to 1.5
Outputs:
- filtered: float32 [128, 262144], P('edges', 'rows')
Inputs may be any that keep to these rules, and one draw needn't show every extreme that they name: `edge_src`: number the devices d = 0 .. 16384 / 32 - 1 along rows and edges together (rows first) and let quarter q be atoms q * 32 to (q + 1) * 32 - 1. Device d holds 1280 edges in order of source atom (cyclically): first the edges of quarter d - 1 it holds, then edges of quarter d, then edges of quarter d + 1 (cyclically over devices). Between 160 and 320 belong to quarter d - 1 and between 160 and 320 to quarter d + 1; for each kind, some device has exactly 320. `edge_dst`: each source, target pair occurs once. The target's tile (atom // 8) lies within 3 tiles of the source's tile, cyclically over 16384 / 8 tiles.
All inputs are finite; a program needn't handle non-finite values.
Results may differ from a plain program's by a relative error of at most 0.0065.
Values may be sent and summed in bfloat16 or wider, within the bound.
A program may use at most 64 MiB of HBM per device.

v0:
```python
import jax
import jax.numpy as jnp
from jax import lax
from jax.sharding import PartitionSpec as P

ORB = 16
TILE_ATOMS = 8
BAND = 3
HID = 256
VEC = 128
STEPS = 4
ATOM_Q = 32
SPILL = 320


def with_halo(x, sides, width):
    for axis, dim in sides:
        devices, length = (lax.axis_size(axis), x.shape[dim])
        up = [(i, (i + 1) % devices) for i in range(devices)]
        down = [(j, i) for i, j in up]
        last = lax.slice_in_dim(x, length - width, length, axis=dim)
        leading = lax.slice_in_dim(x, 0, width, axis=dim)
        before = lax.ppermute(last, axis, up)
        after = lax.ppermute(leading, axis, down)
        x = jnp.concatenate([before, x, after], axis=dim)
    return x


def pair_blocks(feat, cell, cell_bias, w_in, w_out):
    onehot = (cell[:, None] == jnp.arange(3, dtype=jnp.int32)[None, :]).astype(jnp.bfloat16)
    pre = jnp.dot(feat, w_in, preferred_element_type=jnp.float32) + jnp.dot(
        onehot, cell_bias, preferred_element_type=jnp.float32
    )
    hidden = (jax.nn.silu(pre[:, :HID]) * pre[:, HID:]).astype(jnp.bfloat16)
    return jnp.dot(hidden, w_out, preferred_element_type=jnp.float32).astype(jnp.bfloat16)


def per_device(features, edge_src, edge_dst, edge_cell, cell_bias, w_in, w_out, vectors, cheb_coef):
    nquart = lax.axis_size("rows") * lax.axis_size("edges")
    quarter = lax.axis_index("rows") * lax.axis_size("edges") + lax.axis_index("edges")
    ntiles = ATOM_Q * nquart // TILE_ATOMS
    nband = 2 * BAND + 1
    trows = ATOM_Q // TILE_ATOMS
    tile_size = TILE_ATOMS * ORB
    window = nband * TILE_ATOMS * TILE_ATOMS
    id_rows = jnp.stack([edge_src, edge_dst, edge_cell])
    wide_ids = with_halo(id_rows, ((("rows", "edges"), 1),), SPILL)
    source = wide_ids[0]
    target = wide_ids[1]
    cells = wide_ids[2]
    wide_feat = with_halo(features, ((("rows", "edges"), 0),), SPILL)
    blocks = pair_blocks(wide_feat, cells, cell_bias, w_in, w_out)
    total_len = source.shape[0]
    owner = source // ATOM_Q
    mine = owner == quarter
    local_atom = source - quarter * ATOM_Q
    shift_tile = (target // TILE_ATOMS - source // TILE_ATOMS + BAND) % ntiles
    within = (shift_tile * TILE_ATOMS + local_atom % TILE_ATOMS) * TILE_ATOMS + target % TILE_ATOMS
    slot_ids = local_atom // TILE_ATOMS * window + within
    ranks = jnp.cumsum(mine.astype(jnp.int32)) - 1
    dest = jnp.where(mine, ranks, total_len + window)
    packed_blocks = (
        jnp.zeros((total_len + window, ORB * ORB), jnp.bfloat16).at[dest].set(blocks, mode="drop")
    )
    packed_ids = jnp.full((total_len + window,), -1, jnp.int32).at[dest].set(slot_ids, mode="drop")
    tile_first = jnp.arange(trows, dtype=jnp.int32) * TILE_ATOMS
    earlier = jnp.logical_and(mine[None, :], local_atom[None, :] < tile_first[:, None])
    starts = jnp.sum(earlier.astype(jnp.int32), axis=1)

    def one_row(tile_row, start):
        piece = lax.dynamic_slice_in_dim(packed_blocks, start, window, 0)
        piece_ids = lax.dynamic_slice_in_dim(packed_ids, start, window, 0)
        wanted = tile_row * window + jnp.arange(window, dtype=jnp.int32)
        onehot = (wanted[:, None] == piece_ids[None, :]).astype(jnp.bfloat16)
        return jnp.dot(onehot, piece, preferred_element_type=jnp.float32).astype(jnp.bfloat16)

    band = jax.vmap(one_row)(jnp.arange(trows, dtype=jnp.int32), starts)
    band = band.reshape(trows, nband, TILE_ATOMS, TILE_ATOMS, ORB, ORB).transpose(0, 1, 2, 4, 3, 5)
    band = band.reshape(trows, nband, tile_size, tile_size).astype(jnp.float32)

    def apply(field):
        wide = with_halo(field, ((("rows", "edges"), 1),), BAND * tile_size)
        wide3 = wide.reshape(VEC, trows + 2 * BAND, tile_size)
        total = jnp.zeros((VEC, trows, tile_size), jnp.float32)
        for diag in range(nband):
            total = total + jnp.einsum(
                "vtc,trc->vtr",
                wide3[:, diag : diag + trows],
                band[:, diag],
                precision=lax.Precision.HIGHEST,
            )
        return total.reshape(VEC, trows * tile_size)

    previous = lax.all_to_all(vectors, "edges", split_axis=1, concat_axis=0, tiled=True)
    current = apply(previous)
    result = cheb_coef[0] * previous + cheb_coef[1] * current
    for step in range(2, STEPS + 1):
        following = 2.0 * apply(current) - previous
        result = result + cheb_coef[step] * following
        previous, current = (current, following)
    return lax.all_to_all(result, "edges", split_axis=0, concat_axis=1, tiled=True)


def solution(mesh):
    placed = (
        P(("rows", "edges"), None),
        P(("rows", "edges")),
        P(("rows", "edges")),
        P(("rows", "edges")),
        P(),
        P(),
        P(),
        P("edges", "rows"),
        P(),
    )
    return jax.shard_map(
        per_device, mesh=mesh, in_specs=placed, out_specs=P("edges", "rows"), check_vma=False
    )
```

profile of v0, /device:TPU:6, one launch (start us, length us, event | category | flops | bytes accessed | tf_op | source)
XLA Modules:
  0.0 179.9 jit_solution(16395846106777525828)
XLA Ops:
  2.3 1.9 %collective-permute-start = (s32[3,320]{1,0:T(4,128)S(1)}, s32[3,320]{1,0:T(4,128)S(1)}, u32[]{:S(2)}, u32[]{:S(2)}) collective-permute-start(s32[3,320]{1,0:T(4,128)S(1)} %get-tuple-element.54), channel_id=1, source_target_pairs={{0,1},{1,2},{2,3},{3,4},{4,5},{5,6},{6,7},{7,8},{8,9},{9,10},{10,1... | collective-permute-start | bytes 11528 | tf_op jit(solution)/shard_map/ppermute | solution.py:23
  4.2 3.9 %collective-permute-start.1 = (s32[3,320]{1,0:T(4,128)S(1)}, s32[3,320]{1,0:T(4,128)S(1)}, u32[]{:S(2)}, u32[]{:S(2)}) collective-permute-start(s32[3,320]{1,0:T(4,128)S(1)} %get-tuple-element.53), channel_id=1, source_target_pairs={{1,0},{2,1},{3,2},{4,3},{5,4},{6,5},{7,6},{8,7},{9,8},{10,9},{11,1... | collective-permute-start | bytes 11528 | tf_op jit(solution)/shard_map/ppermute | solution.py:24
  9.1 2.9 %collective-permute-start.2 = (bf16[320,256]{1,0:T(8,128)(2,1)S(1)}, bf16[320,256]{1,0:T(8,128)(2,1)S(1)}, u32[]{:S(2)}, u32[]{:S(2)}) collective-permute-start(bf16[320,256]{1,0:T(8,128)(2,1)S(1)} %get-tuple-element.41), channel_id=1, source_target_pairs={{0,1},{1,2},{2,3},{3,4},{4,5},{5,6},{6,7},{7,8},{8,9},{9,10},{10,1... | collective-permute-start | bytes 491528 | tf_op jit(solution)/shard_map/ppermute | solution.py:23
  12.0 3.0 %collective-permute-start.3 = (bf16[320,256]{1,0:T(8,128)(2,1)S(1)}, bf16[320,256]{1,0:T(8,128)(2,1)S(1)}, u32[]{:S(2)}, u32[]{:S(2)}) collective-permute-start(bf16[320,256]{1,0:T(8,128)(2,1)S(1)} %get-tuple-element.42), channel_id=1, source_target_pairs={{1,0},{2,1},{3,2},{4,3},{5,4},{6,5},{7,6},{8,7},{9,8},{10,9},{11,1... | collective-permute-start | bytes 491528 | tf_op jit(solution)/shard_map/ppermute | solution.py:24
  16.7 20.6 %all-to-all-start = ((f32[32,4,512]{2,0,1:T(8,128)}), f32[32,4,512]{2,0,1:T(8,128)S(1)}, u32[]{:S(2)}, u32[]{:S(2)}) async-start(f32[32,4,512]{2,0,1:T(8,128)} %bitcast.143), calls=%async_computation | async-start | bytes 524288 | tf_op jit(solution)/shard_map/all_to_all | solution.py:94
  38.5 10.0 %scatter_custom_fusion = s32[2368]{0:T(1024)S(1)} fusion(s32[1920]{0:T(1024)S(1)} %fusion.80, s32[1920]{0:T(1024)S(1)} %fusion.62, s32[]{:T(128)} %constant.89.clone.1), kind=kCustom, calls=%fused_computation.174 | custom fusion | bytes 9476 | tf_op jit(solution)/shard_map/scatter | solution.py:65
  48.5 5.8 %while.2 = (s32[]{:T(128)}, s32[2368]{0:T(1024)S(1)}, s32[4,1]{0,1:T(1,128)S(1)}, s32[4,448]{1,0:T(4,128)S(1)}, s32[]{:T(128)}, /*index=5*/s32[]{:T(128)}) while((s32[]{:T(128)}, s32[2368]{0:T(1024)S(1)}, s32[4,1]{0,1:T(1,128)S(1)}, s32[4,448]{1,0:T(4,128)S(1)}, s32[]{:T(128)}, /*index=5*/s32[]{:T(128)}) %tuple.45), condition=%wide.while_cond, body=%wide.while_body.sunk | while | flops 2 | bytes 7257 | solution.py:72
  57.1 11.0 %scatter_custom_fusion.1 = bf16[2368,256]{1,0:T(8,128)(2,1)S(1)} fusion(s32[1920]{0:T(1024)S(1)} %fusion.80, bf16[1920,256]{1,0:T(8,128)(2,1)S(1)} %convolution_convert_fusion, bf16[]{:T(256)} %constant.105.clone.1), kind=kCustom, calls=%fused_computation.53 | custom fusion | bytes 1212418 | tf_op jit(solution)/shard_map/scatter | solution.py:63
  68.1 8.3 %while.3 = (s32[]{:T(128)}, bf16[2368,256]{1,0:T(8,128)(2,1)S(1)}, s32[4,2]{0,1:T(2,128)S(1)}, bf16[4,448,256]{2,1,0:T(8,128)(2,1)}, s32[]{:T(128)}) while((s32[]{:T(128)}, bf16[2368,256]{1,0:T(8,128)(2,1)S(1)}, s32[4,2]{0,1:T(2,128)S(1)}, bf16[4,448,256]{2,1,0:T(8,128)(2,1)}, s32[]{:T(128)}) %tuple.42), condition=%wide.while_cond.1, body=%wide.while_body.1.sunk | while | flops 2 | bytes 459865 | solution.py:71
  76.5 1.9 %collective-permute-start.4 = (f32[128,384]{1,0:T(8,128)S(1)}, f32[128,384]{1,0:T(8,128)S(1)}, u32[]{:S(2)}, u32[]{:S(2)}) collective-permute-start(f32[128,384]{1,0:T(8,128)S(1)} %get-tuple-element.51), channel_id=1, source_target_pairs={{0,1},{1,2},{2,3},{3,4},{4,5},{5,6},{6,7},{7,8},{8,9},{9,10},{10,1... | collective-permute-start | bytes 589832 | tf_op jit(solution)/shard_map/ppermute | solution.py:23
  78.4 4.1 %collective-permute-start.5 = (f32[128,384]{1,0:T(8,128)S(1)}, f32[128,384]{1,0:T(8,128)S(1)}, u32[]{:S(2)}, u32[]{:S(2)}) collective-permute-start(f32[128,384]{1,0:T(8,128)S(1)} %get-tuple-element.52), channel_id=1, source_target_pairs={{1,0},{2,1},{3,2},{4,3},{5,4},{6,5},{7,6},{8,7},{9,8},{10,9},{11,1... | collective-permute-start | bytes 589832 | tf_op jit(solution)/shard_map/ppermute | solution.py:24
  84.4 6.8 %reshape.221 = bf16[4,7,8,8,16,16]{5,4,3,2,1,0:T(8,128)(2,1)} reshape(bf16[4,448,256]{2,1,0:T(8,128)(2,1)S(1)} %fusion.5) | data formatting | bytes 1835008 | tf_op jit(solution)/shard_map/reshape | solution.py:78
  91.2 9.8 %copy.129 = bf16[4,7,8,16,8,16]{5,4,3,2,0,1:T(8,128)(2,1)} copy(bf16[4,7,8,16,8,16]{5,3,4,2,1,0:T(8,128)(2,1)} %bitcast.152) | data formatting | bytes 1835008 | tf_op jit(solution)/shard_map/transpose | solution.py:78
  101.0 8.1 %reshape.222 = bf16[4,7,128,128]{3,2,0,1:T(8,128)(2,1)S(1)} reshape(bf16[4,7,8,16,8,16]{5,4,3,2,0,1:T(8,128)(2,1)} %copy.129) | data formatting | bytes 1835008 | tf_op jit(solution)/shard_map/reshape | solution.py:79
  111.5 2.9 %collective-permute-start.6 = (f32[128,384]{0,1:T(8,128)S(1)}, f32[128,384]{0,1:T(8,128)S(1)}, u32[]{:S(2)}, u32[]{:S(2)}) collective-permute-start(f32[128,384]{0,1:T(8,128)S(1)} %get-tuple-element.49), channel_id=1, source_target_pairs={{0,1},{1,2},{2,3},{3,4},{4,5},{5,6},{6,7},{7,8},{8,9},{9,10},{10,1... | collective-permute-start | bytes 589832 | tf_op jit(solution)/shard_map/ppermute | solution.py:23
  114.3 3.0 %collective-permute-start.7 = (f32[128,384]{0,1:T(8,128)S(1)}, f32[128,384]{0,1:T(8,128)S(1)}, u32[]{:S(2)}, u32[]{:S(2)}) collective-permute-start(f32[128,384]{0,1:T(8,128)S(1)} %get-tuple-element.50), channel_id=1, source_target_pairs={{1,0},{2,1},{3,2},{4,3},{5,4},{6,5},{7,6},{8,7},{9,8},{10,9},{11,1... | collective-permute-start | bytes 589832 | tf_op jit(solution)/shard_map/ppermute | solution.py:24
  119.0 4.5 %collective-permute-done.7 = f32[128,384]{0,1:T(8,128)S(1)} collective-permute-done((f32[128,384]{0,1:T(8,128)S(1)}, f32[128,384]{0,1:T(8,128)S(1)}, u32[]{:S(2)}, u32[]{:S(2)}) %collective-permute-start.7) | collective-permute-done | bytes 196640 | tf_op jit(solution)/shard_map/ppermute | solution.py:24
  125.8 1.9 %collective-permute-start.8 = (f32[128,384]{1,0:T(8,128)S(1)}, f32[128,384]{1,0:T(8,128)S(1)}, u32[]{:S(2)}, u32[]{:S(2)}) collective-permute-start(f32[128,384]{1,0:T(8,128)S(1)} %get-tuple-element.47), channel_id=1, source_target_pairs={{0,1},{1,2},{2,3},{3,4},{4,5},{5,6},{6,7},{7,8},{8,9},{9,10},{10,1... | collective-permute-start | bytes 589832 | tf_op jit(solution)/shard_map/ppermute | solution.py:23
  127.7 4.1 %collective-permute-start.9 = (f32[128,384]{1,0:T(8,128)S(1)}, f32[128,384]{1,0:T(8,128)S(1)}, u32[]{:S(2)}, u32[]{:S(2)}) collective-permute-start(f32[128,384]{1,0:T(8,128)S(1)} %get-tuple-element.48), channel_id=1, source_target_pairs={{1,0},{2,1},{3,2},{4,3},{5,4},{6,5},{7,6},{8,7},{9,8},{10,9},{11,1... | collective-permute-start | bytes 589832 | tf_op jit(solution)/shard_map/ppermute | solution.py:24
  133.4 4.7 %collective-permute-done.9 = f32[128,384]{1,0:T(8,128)S(1)} collective-permute-done((f32[128,384]{1,0:T(8,128)S(1)}, f32[128,384]{1,0:T(8,128)S(1)}, u32[]{:S(2)}, u32[]{:S(2)}) %collective-permute-start.9) | collective-permute-done | bytes 196640 | tf_op jit(solution)/shard_map/ppermute | solution.py:24
  144.4 3.9 %collective-permute-start.11 = (f32[128,384]{0,1:T(8,128)}, f32[128,384]{0,1:T(8,128)}, u32[]{:S(2)}, u32[]{:S(2)}) collective-permute-start(f32[128,384]{0,1:T(8,128)} %get-tuple-element.44), channel_id=1, source_target_pairs={{1,0},{2,1},{3,2},{4,3},{5,4},{6,5},{7,6},{8,7},{9,8},{10,9},{11,1... | collective-permute-start | bytes 589832 | tf_op jit(solution)/shard_map/ppermute | solution.py:24
  150.4 4.7 %collective-permute-done.11 = f32[128,384]{0,1:T(8,128)} collective-permute-done((f32[128,384]{0,1:T(8,128)}, f32[128,384]{0,1:T(8,128)}, u32[]{:S(2)}, u32[]{:S(2)}) %collective-permute-start.11) | collective-permute-done | bytes 196640 | tf_op jit(solution)/shard_map/ppermute | solution.py:24
  158.4 2.0 %fusion.58 = f32[4,32,512]{2,1,0:T(8,128)S(1)} fusion(f32[4,32,512]{2,1,0:T(8,128)S(1)} %mul.128, f32[4,32,512]{2,1,0:T(8,128)S(1)} %mul.119, f32[32,4,512]{2,0,1:T(8,128)S(1)} %all-to-all-done, f32[4,32,512]{2,1,0:T(8,128)S(1)} %mul.132, f32[4,32,512]{2,1,0:T(8,128)S(1)} %mul.122, f32[]{:T(128)} %bitcast.26, f32[]{:T(128)} %bitcast.17, f32[]{:T(128)} %bitcast), kind=kLoop, calls=%fused_computation.98 | loop fusion | flops 589824 | bytes 1572876 | tf_op jit(solution)/shard_map/add | solution.py:99
  160.5 18.7 %all_to_all.35 = f32[4,32,512]{2,1,0:T(8,128)S(1)} all-to-all(f32[4,32,512]{2,1,0:T(8,128)S(1)} %fusion.58), channel_id=1, replica_groups=mesh['rows'=128,'edges'=4] {'edges'}, dimensions={0} | all-to-all | bytes 524288 | tf_op jit(solution)/shard_map/all_to_all | solution.py:101
  (126 shorter events, 44.8 us)
Async XLA Ops:
  0.0 55.6 %copy-start = (bf16[256,512]{1,0:T(8,128)(2,1)S(1)}, bf16[256,512]{1,0:T(8,128)(2,1)}, u32[]{:S(2)}) copy-start(bf16[256,512]{1,0:T(8,128)(2,1)} %param.14) | copy-start | bytes 786436
  0.0 54.3 %copy-start.3 = (bf16[3,512]{1,0:T(4,128)(2,1)S(1)}, bf16[3,512]{1,0:T(4,128)(2,1)}, u32[]{:S(2)}) copy-start(bf16[3,512]{1,0:T(4,128)(2,1)} %param.13) | copy-start | bytes 9220
  2.3 35.1 %collective-permute-start = (s32[3,320]{1,0:T(4,128)S(1)}, s32[3,320]{1,0:T(4,128)S(1)}, u32[]{:S(2)}, u32[]{:S(2)}) collective-permute-start(s32[3,320]{1,0:T(4,128)S(1)} %get-tuple-element.54), channel_id=1, source_target_pairs={{0,1},{1,2},{2,3},{3,4},{4,5},{5,6},{6,7},{7,8},{8,9},{9,10},{10,1... | collective-permute-start | bytes 11528 | tf_op jit(solution)/shard_map/ppermute | solution.py:23
  4.2 33.1 %collective-permute-start.1 = (s32[3,320]{1,0:T(4,128)S(1)}, s32[3,320]{1,0:T(4,128)S(1)}, u32[]{:S(2)}, u32[]{:S(2)}) collective-permute-start(s32[3,320]{1,0:T(4,128)S(1)} %get-tuple-element.53), channel_id=1, source_target_pairs={{1,0},{2,1},{3,2},{4,3},{5,4},{6,5},{7,6},{8,7},{9,8},{10,9},{11,1... | collective-permute-start | bytes 11528 | tf_op jit(solution)/shard_map/ppermute | solution.py:24
  9.1 46.4 %collective-permute-start.2 = (bf16[320,256]{1,0:T(8,128)(2,1)S(1)}, bf16[320,256]{1,0:T(8,128)(2,1)S(1)}, u32[]{:S(2)}, u32[]{:S(2)}) collective-permute-start(bf16[320,256]{1,0:T(8,128)(2,1)S(1)} %get-tuple-element.41), channel_id=1, source_target_pairs={{0,1},{1,2},{2,3},{3,4},{4,5},{5,6},{6,7},{7,8},{8,9},{9,10},{10,1... | collective-permute-start | bytes 491528 | tf_op jit(solution)/shard_map/ppermute | solution.py:23
  12.0 43.6 %collective-permute-start.3 = (bf16[320,256]{1,0:T(8,128)(2,1)S(1)}, bf16[320,256]{1,0:T(8,128)(2,1)S(1)}, u32[]{:S(2)}, u32[]{:S(2)}) collective-permute-start(bf16[320,256]{1,0:T(8,128)(2,1)S(1)} %get-tuple-element.42), channel_id=1, source_target_pairs={{1,0},{2,1},{3,2},{4,3},{5,4},{6,5},{7,6},{8,7},{9,8},{10,9},{11,1... | collective-permute-start | bytes 491528 | tf_op jit(solution)/shard_map/ppermute | solution.py:24
  16.7 59.8 %all-to-all-start = ((f32[32,4,512]{2,0,1:T(8,128)}), f32[32,4,512]{2,0,1:T(8,128)S(1)}, u32[]{:S(2)}, u32[]{:S(2)}) async-start(f32[32,4,512]{2,0,1:T(8,128)} %bitcast.143), calls=%async_computation | async-start | bytes 524288 | tf_op jit(solution)/shard_map/all_to_all | solution.py:94
  54.4 1.3 copy-start.1
  55.6 0.9 copy-start.4
  76.5 32.7 %collective-permute-start.4 = (f32[128,384]{1,0:T(8,128)S(1)}, f32[128,384]{1,0:T(8,128)S(1)}, u32[]{:S(2)}, u32[]{:S(2)}) collective-permute-start(f32[128,384]{1,0:T(8,128)S(1)} %get-tuple-element.51), channel_id=1, source_target_pairs={{0,1},{1,2},{2,3},{3,4},{4,5},{5,6},{6,7},{7,8},{8,9},{9,10},{10,1... | collective-permute-start | bytes 589832 | tf_op jit(solution)/shard_map/ppermute | solution.py:23
  78.4 30.8 %collective-permute-start.5 = (f32[128,384]{1,0:T(8,128)S(1)}, f32[128,384]{1,0:T(8,128)S(1)}, u32[]{:S(2)}, u32[]{:S(2)}) collective-permute-start(f32[128,384]{1,0:T(8,128)S(1)} %get-tuple-element.52), channel_id=1, source_target_pairs={{1,0},{2,1},{3,2},{4,3},{5,4},{6,5},{7,6},{8,7},{9,8},{10,9},{11,1... | collective-permute-start | bytes 589832 | tf_op jit(solution)/shard_map/ppermute | solution.py:24
  111.5 7.6 %collective-permute-start.6 = (f32[128,384]{0,1:T(8,128)S(1)}, f32[128,384]{0,1:T(8,128)S(1)}, u32[]{:S(2)}, u32[]{:S(2)}) collective-permute-start(f32[128,384]{0,1:T(8,128)S(1)} %get-tuple-element.49), channel_id=1, source_target_pairs={{0,1},{1,2},{2,3},{3,4},{4,5},{5,6},{6,7},{7,8},{8,9},{9,10},{10,1... | collective-permute-start | bytes 589832 | tf_op jit(solution)/shard_map/ppermute | solution.py:23
  114.3 9.2 %collective-permute-start.7 = (f32[128,384]{0,1:T(8,128)S(1)}, f32[128,384]{0,1:T(8,128)S(1)}, u32[]{:S(2)}, u32[]{:S(2)}) collective-permute-start(f32[128,384]{0,1:T(8,128)S(1)} %get-tuple-element.50), channel_id=1, source_target_pairs={{1,0},{2,1},{3,2},{4,3},{5,4},{6,5},{7,6},{8,7},{9,8},{10,9},{11,1... | collective-permute-start | bytes 589832 | tf_op jit(solution)/shard_map/ppermute | solution.py:24
  125.0 6.9 %copy-start.2 = (f32[5]{0:T(128)S(1)}, f32[5]{0:T(128)}, u32[]{:S(2)}) copy-start(f32[5]{0:T(128)} %param.17) | copy-start | bytes 64
  125.8 7.6 %collective-permute-start.8 = (f32[128,384]{1,0:T(8,128)S(1)}, f32[128,384]{1,0:T(8,128)S(1)}, u32[]{:S(2)}, u32[]{:S(2)}) collective-permute-start(f32[128,384]{1,0:T(8,128)S(1)} %get-tuple-element.47), channel_id=1, source_target_pairs={{0,1},{1,2},{2,3},{3,4},{4,5},{5,6},{6,7},{7,8},{8,9},{9,10},{10,1... | collective-permute-start | bytes 589832 | tf_op jit(solution)/shard_map/ppermute | solution.py:23
  127.7 10.3 %collective-permute-start.9 = (f32[128,384]{1,0:T(8,128)S(1)}, f32[128,384]{1,0:T(8,128)S(1)}, u32[]{:S(2)}, u32[]{:S(2)}) collective-permute-start(f32[128,384]{1,0:T(8,128)S(1)} %get-tuple-element.48), channel_id=1, source_target_pairs={{1,0},{2,1},{3,2},{4,3},{5,4},{6,5},{7,6},{8,7},{9,8},{10,9},{11,1... | collective-permute-start | bytes 589832 | tf_op jit(solution)/shard_map/ppermute | solution.py:24
  142.5 7.9 %collective-permute-start.10 = (f32[128,384]{0,1:T(8,128)}, f32[128,384]{0,1:T(8,128)}, u32[]{:S(2)}, u32[]{:S(2)}) collective-permute-start(f32[128,384]{0,1:T(8,128)} %get-tuple-element.43), channel_id=1, source_target_pairs={{0,1},{1,2},{2,3},{3,4},{4,5},{5,6},{6,7},{7,8},{8,9},{9,10},{10,1... | collective-permute-start | bytes 589832 | tf_op jit(solution)/shard_map/ppermute | solution.py:23
  144.4 10.6 %collective-permute-start.11 = (f32[128,384]{0,1:T(8,128)}, f32[128,384]{0,1:T(8,128)}, u32[]{:S(2)}, u32[]{:S(2)}) collective-permute-start(f32[128,384]{0,1:T(8,128)} %get-tuple-element.44), channel_id=1, source_target_pairs={{1,0},{2,1},{3,2},{4,3},{5,4},{6,5},{7,6},{8,7},{9,8},{10,9},{11,1... | collective-permute-start | bytes 589832 | tf_op jit(solution)/shard_map/ppermute | solution.py:24
where the time goes:
time: 182 us; the launch traced here: 180 us
  local copies, waits for them, and re-layouts  69 us (38%)
  starting transfers between devices  56 us (31%)
  blocking collectives  18.7 us (10%)
  waiting for transfers between devices  17.5 us (10%)
  matrix products  13.6 us (7%)
  other arithmetic  4.28 us (2%)
    ppermute x6, starting transfers between devices, with_halo(): after = lax.ppermute(leading, axis, down)  22.1 us
    all_to_all x1, starting transfers between devices, per_device(): lax.all_to_all(vectors, 'edges', split_axis=1, concat_axis=0, tiled=True)  20.6 us
    all_to_all x1, blocking collectives, per_device(): lax.all_to_all(result, 'edges', split_axis=0, concat_axis=1, tiled=True)  18.7 us
    gather x24, local copies, waits for them, and re-layouts  14 us
    ppermute x6, waiting for transfers between devices, with_halo(): after = lax.ppermute(leading, axis, down)  13.8 us
    ppermute x6, starting transfers between devices, with_halo(): before = lax.ppermute(last, axis, up)  13.4 us
    scatter x1, local copies, waits for them, and re-layouts, per_device(): jnp.zeros((total_len + window, ORB * ORB), jnp.bfloat16).at[dest]  11 us
    scatter x1, local copies, waits for them, and re-layouts, per_device(): jnp.full((total_len + window,), -1, jnp.int32).at[dest]  9.99 us
  transfers between devices with their start and end apart: 13, of which 6 were waited for; matrix products, arithmetic and copies ran while one was open for 39% of the time, Pallas kernels for 0%

commit v1 on v0

v1 whole, which is shorter than its diff:
```python
import functools

import jax
import jax.numpy as jnp
from jax import lax
from jax.experimental import pallas as pl
from jax.experimental.pallas import tpu as pltpu
from jax.sharding import PartitionSpec as P

MESH = pl.DeviceIdType.MESH
BF16 = jnp.bfloat16
F32 = jnp.float32

ORB = 16
TILE_ATOMS = 8
BAND = 3
NBAND = 2 * BAND + 1
HID = 256
VEC = 128
STEPS = 4
ATOM_Q = 32
SPILL = 320
E_DEV = 1280
TILE = TILE_ATOMS * ORB
TROWS = ATOM_Q // TILE_ATOMS
OWN = TROWS * TILE
HALO = BAND * TILE
WIDE = OWN + 2 * HALO
LANES = 128
IDROWS = E_DEV // LANES
SLOTS_I = TROWS * NBAND * TILE_ATOMS
ENDS = 384
PAD = ENDS - SPILL
GROUPS = 2
GROWS = VEC // GROUPS


def kernel(
    nrows, nedges,
    feat, src, dst, cell, bias, w_in, w_out, vec, coef,
    out,
    fown, fends, ids_own, ids_low, ids_high, bias_v, bias8, win_v, wout_v, wperm, vec_v, vsend,
    slots, blk, cmat, ht32, ht, tw, tf, res,
    loc_sem, ids_send, ids_recv, feat_send, feat_recv, a2a_send, a2a_recv,
    halo_send, halo_recv, fin_send, fin_recv,
):
    r = lax.axis_index("rows")
    x = lax.axis_index("edges")
    quarter = r * nedges + x
    ntiles = nrows * nedges * TROWS
    own_vecs = VEC // nedges

    up_x = lax.rem(x + 1, nedges)
    up_r = lax.rem(r + (x + 1) // nedges, nrows)
    down_x = lax.rem(x + nedges - 1, nedges)
    down_r = lax.rem(r + nrows - 1 + (x + nedges - 1) // nedges, nrows)
    up = (up_r, up_x)
    down = (down_r, down_x)

    def remote(source, target, send, recv, device):
        return pltpu.make_async_remote_copy(
            src_ref=source, dst_ref=target, send_sem=send, recv_sem=recv,
            device_id=device, device_id_type=MESH,
        )

    loads = [
        pltpu.make_async_copy(vec, vec_v, loc_sem.at[0]),
        pltpu.make_async_copy(w_out, wout_v, loc_sem.at[1]),
        pltpu.make_async_copy(w_in, win_v, loc_sem.at[2]),
        pltpu.make_async_copy(bias, bias_v, loc_sem.at[3]),
        pltpu.make_async_copy(feat, fown, loc_sem.at[4]),
        pltpu.make_async_copy(src, ids_own.at[0], loc_sem.at[5]),
        pltpu.make_async_copy(dst, ids_own.at[1], loc_sem.at[6]),
        pltpu.make_async_copy(cell, ids_own.at[2], loc_sem.at[7]),
    ]
    for load in loads:
        load.start()

    barrier = pltpu.get_barrier_semaphore()
    peers = [up, down] + [(r, lax.rem(x + off, nedges)) for off in range(1, nedges)]
    for peer in peers:
        pl.semaphore_signal(barrier, inc=1, device_id=peer, device_id_type=MESH)

    loads[0].wait()
    vsend[...] = vec_v[...].astype(BF16)
    own_cols = pl.ds(pl.multiple_of(x * OWN, OWN), OWN)
    own_rows = pl.ds(pl.multiple_of(x * own_vecs, own_vecs), own_vecs)
    tw[0, own_rows, HALO : HALO + OWN] = vec_v[:, own_cols].astype(BF16)
    fends[0:PAD, :] = jnp.zeros((PAD, HID), BF16)
    fends[2 * ENDS - PAD : 2 * ENDS, :] = jnp.zeros((PAD, HID), BF16)

    pl.semaphore_wait(barrier, len(peers))

    id_copies = []
    for n, ref in enumerate((src, dst, cell)):
        id_copies.append(remote(ref, ids_low.at[n], ids_send.at[0, n], ids_recv.at[0, n], up))
        id_copies.append(remote(ref, ids_high.at[n], ids_send.at[1, n], ids_recv.at[1, n], down))
    feat_copies = [
        remote(feat.at[E_DEV - SPILL : E_DEV], fends.at[PAD:ENDS], feat_send.at[0], feat_recv.at[0], up),
        remote(feat.at[0:SPILL], fends.at[ENDS : ENDS + SPILL], feat_send.at[1], feat_recv.at[1], down),
    ]
    for copy in id_copies + feat_copies:
        copy.start()
    a2a_copies = []
    for off in range(1, nedges):
        to = lax.rem(x + off, nedges)
        cols = pl.ds(pl.multiple_of(to * OWN, OWN), OWN)
        a2a_copies.append(
            remote(
                vsend.at[:, cols], tw.at[0, own_rows, HALO : HALO + OWN],
                a2a_send.at[off], a2a_recv.at[off], (r, to),
            )
        )
    for copy in a2a_copies:
        copy.start()

    loads[1].wait()
    k_id = lax.broadcasted_iota(jnp.int32, (HID, HID), 0)
    n_id = lax.broadcasted_iota(jnp.int32, (HID, HID), 1)
    swap = jnp.logical_and(n_id // ORB == k_id % ORB, n_id % ORB == k_id // ORB)
    perm = jnp.where(swap, 1.0, 0.0).astype(BF16)
    wperm[...] = jnp.dot(wout_v[...], perm, preferred_element_type=F32).astype(BF16)
    for load in loads[2:]:
        load.wait()
    bias8[...] = jnp.zeros_like(bias8)
    bias8[0:3, :] = bias_v[...].astype(F32)

    sub8 = lax.broadcasted_iota(jnp.int32, (8, LANES), 0)

    def pair_net(features, cell_rows, target):
        onehot = jnp.concatenate(
            [jnp.where(row == sub8, 1.0, 0.0) for row in cell_rows], axis=1
        )
        pre = jnp.dot(features, win_v[...], preferred_element_type=F32)
        pre = pre + lax.dot_general(
            onehot.astype(BF16), bias8[...].astype(BF16), (((0,), (0,)), ((), ())),
            preferred_element_type=F32,
        )
        gate = pre[:, :HID]
        hidden = (0.5 * gate * (1.0 + jnp.tanh(0.5 * gate)) * pre[:, HID:]).astype(BF16)
        target[...] = jnp.dot(hidden, wperm[...], preferred_element_type=F32).astype(BF16)

    def slot_ids(ids):
        source = ids[0]
        goal = ids[1]
        local = source % ATOM_Q
        shift = goal // TILE_ATOMS - source // TILE_ATOMS + BAND
        shift = jnp.where(shift < 0, shift + ntiles, shift)
        shift = jnp.where(shift >= ntiles, shift - ntiles, shift)
        slot = (
            (local % TILE_ATOMS) * SLOTS_I
            + (local // TILE_ATOMS * NBAND + shift) * TILE_ATOMS
            + goal % TILE_ATOMS
        )
        return jnp.where(source // ATOM_Q == quarter, slot, -1)

    for c in range(IDROWS // 2):
        rows = slice(2 * c * LANES, (2 * c + 2) * LANES)
        cell_rows = [ids_own[2, n : n + 1, :] for n in (2 * c, 2 * c + 1)]
        pair_net(fown[rows, :], cell_rows, blk.at[rows])
    own_slots = slot_ids(ids_own)
    for c in range(IDROWS):
        slots[:, c * LANES : (c + 1) * LANES] = own_slots[c : c + 1, :]

    place = lax.broadcasted_iota(jnp.int32, (SLOTS_I, 1), 0)

    def choose(i, start, count):
        row = slots[:, start : start + count] - i * SLOTS_I
        onehot = jnp.where(row == place, 1.0, 0.0).astype(BF16)
        return jnp.dot(onehot, blk[start : start + count, :], preferred_element_type=F32)

    @pl.loop(0, TILE_ATOMS)
    def _(i):
        cmat[i] = choose(i, 0, E_DEV)

    for copy in a2a_copies:
        copy.wait_recv()

    def halo(step, group, rows):
        return [
            remote(
                tw.at[step, rows, HALO + OWN - HALO : HALO + OWN], tw.at[step, rows, 0:HALO],
                halo_send.at[step, 0, group], halo_recv.at[step, 0, group], up,
            ),
            remote(
                tw.at[step, rows, HALO : 2 * HALO], tw.at[step, rows, HALO + OWN : WIDE],
                halo_send.at[step, 1, group], halo_recv.at[step, 1, group], down,
            ),
        ]

    group_rows = [slice(g * GROWS, (g + 1) * GROWS) for g in range(GROUPS)]
    halos = {}
    for g in range(GROUPS):
        halos[0, g] = halo(0, g, group_rows[g])
        for copy in halos[0, g]:
            copy.start()

    for copy in id_copies + feat_copies:
        copy.wait_recv()
    low_slots = slot_ids(ids_low)
    high_slots = slot_ids(ids_high)
    nends = ENDS // LANES
    for c in range(nends):
        at = E_DEV + c * LANES
        slots[:, at : at + LANES] = low_slots[IDROWS - nends + c : IDROWS - nends + c + 1, :]
        at = at + ENDS
        slots[:, at : at + LANES] = high_slots[c : c + 1, :]
    end_cells = [ids_low[2, n : n + 1, :] for n in range(IDROWS - nends, IDROWS)]
    end_cells += [ids_high[2, n : n + 1, :] for n in range(nends)]
    for c in range(nends):
        rows = slice(2 * c * LANES, (2 * c + 2) * LANES)
        target = blk.at[E_DEV + 2 * c * LANES : E_DEV + (2 * c + 2) * LANES]
        pair_net(fends[rows, :], end_cells[2 * c : 2 * c + 2], target)

    @pl.loop(0, TILE_ATOMS)
    def _(i):
        cmat[i] = cmat[i] + choose(i, E_DEV, 2 * ENDS)

    lane = lax.broadcasted_iota(jnp.int32, (8, LANES), 1)

    @pl.loop(0, TROWS * NBAND)
    def _(td):
        start = td * TILE
        rows = pl.ds(pl.multiple_of(td * 8, 8), 8)
        for half in range(2):
            parts = [cmat[i, rows, half * LANES : (half + 1) * LANES] for i in range(8)]
            for bit in range(3):
                width = ORB << bit
                high_lane = (lane // width) % 2 == 1
                for n in range(8):
                    if n & (1 << bit):
                        continue
                    m = n | (1 << bit)
                    first = jnp.where(high_lane, pltpu.roll(parts[m], width, 1), parts[n])
                    second = jnp.where(high_lane, parts[m], pltpu.roll(parts[n], LANES - width, 1))
                    parts[n], parts[m] = first, second
            for n in range(8):
                ht32[pl.ds(start + half * 8 + n, 8, stride=ORB), :] = parts[n]

    for pair in range(TROWS // 2):
        ht[pair, NBAND * TILE : (NBAND + 1) * TILE, 0:TILE] = jnp.zeros((TILE, TILE), BF16)
        ht[pair, 0:TILE, TILE : 2 * TILE] = jnp.zeros((TILE, TILE), BF16)
        for a in range(2):
            t = 2 * pair + a
            piece = ht32[t * NBAND * TILE : (t + 1) * NBAND * TILE, :].astype(BF16)
            ht[pair, a * TILE : (a + NBAND) * TILE, a * TILE : (a + 1) * TILE] = piece

    finals = []
    for step in range(1, STEPS + 1):
        for g in range(GROUPS):
            rows = group_rows[g]
            for copy in halos[step - 1, g]:
                copy.wait_recv()
            for pair in range(TROWS // 2):
                cols = slice(pair * 2 * TILE, (pair + 1) * 2 * TILE)
                wide = slice(pair * 2 * TILE, pair * 2 * TILE + (NBAND + 1) * TILE)
                product = jnp.dot(tw[step - 1, rows, wide], ht[pair], preferred_element_type=F32)
                mid = slice(HALO + pair * 2 * TILE, HALO + (pair + 1) * 2 * TILE)
                if step == 1:
                    new = product
                    total = coef[0] * tw[0, rows, mid].astype(F32) + coef[1] * new
                else:
                    if step == 2:
                        older = tw[0, rows, mid].astype(F32)
                    else:
                        older = tf[step - 3, rows, cols]
                    new = 2.0 * product - older
                    total = res[rows, cols] + coef[step] * new
                if step < STEPS:
                    tw[step, rows, mid] = new.astype(BF16)
                if step < STEPS - 1:
                    tf[step - 1, rows, cols] = new
                if step < STEPS:
                    res[rows, cols] = total
                else:
                    fsend = tw.at[STEPS]
                    fsend[rows, cols] = total.astype(BF16)
            if step < STEPS:
                halos[step, g] = halo(step, g, rows)
                for copy in halos[step, g]:
                    copy.start()
            else:
                for owner in range(g * GROWS // own_vecs, (g + 1) * GROWS // own_vecs):
                    vecs = slice(owner * own_vecs, (owner + 1) * own_vecs)
                    copy = remote(
                        tw.at[STEPS, vecs, 0:OWN], out.at[:, own_cols],
                        fin_send.at[owner], fin_recv.at[x], (r, owner),
                    )
                    finals.append(copy)

                    @pl.when(x != owner)
                    def _(copy=copy):
                        copy.start()

                    @pl.when(x == owner)
                    def _(vecs=vecs):
                        out[:, own_cols] = tw[STEPS, vecs, 0:OWN]

    for copy in id_copies + feat_copies + a2a_copies:
        copy.wait_send()
    for pair in halos.values():
        for copy in pair:
            copy.wait_send()
    for owner in range(nedges):

        @pl.when(x != owner)
        def _(owner=owner):
            finals[owner].wait_send()
            remote(
                tw.at[STEPS, 0:own_vecs, 0:OWN], out.at[:, owner * OWN : (owner + 1) * OWN],
                fin_send.at[owner], fin_recv.at[owner], (r, owner),
            ).wait_recv()


def per_device(nrows, nedges, features, edge_src, edge_dst, edge_cell, cell_bias, w_in, w_out, vectors, cheb_coef):
    ids = [a.reshape(IDROWS, LANES) for a in (edge_src, edge_dst, edge_cell)]
    own_vecs = VEC // nedges
    dma = pltpu.SemaphoreType.DMA
    anywhere = pl.BlockSpec(memory_space=pl.ANY)
    result = pl.pallas_call(
        functools.partial(kernel, nrows, nedges),
        out_shape=jax.ShapeDtypeStruct(vectors.shape, BF16),
        in_specs=[anywhere] * 8 + [pl.BlockSpec(memory_space=pltpu.SMEM)],
        out_specs=pl.BlockSpec(memory_space=pltpu.VMEM),
        scratch_shapes=[
            pltpu.VMEM((E_DEV, HID), BF16),
            pltpu.VMEM((2 * ENDS, HID), BF16),
            pltpu.VMEM((3, IDROWS, LANES), jnp.int32),
            pltpu.VMEM((3, IDROWS, LANES), jnp.int32),
            pltpu.VMEM((3, IDROWS, LANES), jnp.int32),
            pltpu.VMEM((3, 2 * HID), BF16),
            pltpu.VMEM((8, 2 * HID), F32),
            pltpu.VMEM((HID, 2 * HID), BF16),
            pltpu.VMEM((HID, HID), BF16),
            pltpu.VMEM((HID, HID), BF16),
            pltpu.VMEM(vectors.shape, F32),
            pltpu.VMEM(vectors.shape, BF16),
            pltpu.VMEM((1, E_DEV + 2 * ENDS), jnp.int32),
            pltpu.VMEM((E_DEV + 2 * ENDS, HID), BF16),
            pltpu.VMEM((TILE_ATOMS, SLOTS_I, HID), F32),
            pltpu.VMEM((TROWS * NBAND * TILE, TILE), F32),
            pltpu.VMEM((TROWS // 2, (NBAND + 1) * TILE, 2 * TILE), BF16),
            pltpu.VMEM((STEPS + 1, VEC, WIDE), BF16),
            pltpu.VMEM((STEPS - 2, VEC, OWN), F32),
            pltpu.VMEM((VEC, OWN), F32),
            dma((8,)),
            dma((2, 3)),
            dma((2, 3)),
            dma((2,)),
            dma((2,)),
            dma((nedges,)),
            dma((nedges,)),
            dma((STEPS, 2, GROUPS)),
            dma((STEPS, 2, GROUPS)),
            dma((nedges,)),
            dma((nedges,)),
        ],
        compiler_params=pltpu.CompilerParams(
            collective_id=0, has_side_effects=True
        ),
        name="filter",
    )(features, *ids, cell_bias, w_in, w_out, vectors, cheb_coef)
    return result.astype(F32)


def solution(mesh):
    nrows, nedges = mesh.shape["rows"], mesh.shape["edges"]
    placed = (
        P(("rows", "edges"), None),
        P(("rows", "edges")),
        P(("rows", "edges")),
        P(("rows", "edges")),
        P(),
        P(),
        P(),
        P("edges", "rows"),
        P(),
    )
    return jax.shard_map(
        functools.partial(per_device, nrows, nedges),
        mesh=mesh,
        in_specs=placed,
        out_specs=P("edges", "rows"),
        check_vma=False,
    )
```

time: 182 us -> 55.1 us (0.30); the launches traced: 180 us -> 54.9 us
  local copies, waits for them, and re-layouts: 69 us -> 0 us
  starting transfers between devices: 56 us -> 0 us
  Pallas kernels: 0 us -> 53.3 us
  blocking collectives: 18.7 us -> 0 us
  waiting for transfers between devices: 17.5 us -> 0 us
  matrix products: 13.6 us -> 0 us
  other arithmetic: 4.28 us -> 1.63 us
    pallas_call x0 -> x1, Pallas kernels: none -> 53.3 us  [per_device(): pl.pallas_call(functools.partial(kernel, nrows, nedges), out_shape=jax.Sh...]
    ppermute x12 -> x0, starting transfers between devices: 35.4 us -> none  [the longest x6 22.1 us: with_halo(): after = lax.ppermute(leading, axis, down)]
    scatter x2 -> x0, local copies, waits for them, and re-layouts: 21 us -> none  [the longest x1 11 us: per_device(): jnp.zeros((total_len + window, ORB * ORB), jnp.bfloat16).at[dest]]
    all_to_all x1 -> x0, starting transfers between devices: 20.6 us -> none  [per_device(): lax.all_to_all(vectors, 'edges', split_axis=1, concat_axis=0, tiled=True)]
    all_to_all x1 -> x0, blocking collectives: 18.7 us -> none  [per_device(): lax.all_to_all(result, 'edges', split_axis=0, concat_axis=1, tiled=True)]
    ppermute x12 -> x0, waiting for transfers between devices: 17.5 us -> none  [the longest x6 13.8 us: with_halo(): after = lax.ppermute(leading, axis, down)]
    reshape x2 -> x0, local copies, waits for them, and re-layouts: 14.9 us -> none  [the longest x1 8.1 us: per_device(): band = band.reshape(trows, nband, tile_size, tile_size).astype(jnp.float32)]
    gather x24 -> x0, local copies, waits for them, and re-layouts: 14 us -> none
  transfers between devices with their start and end apart: 13 -> 0, of which waited for: 6 -> 0; matrix products, arithmetic and copies ran while one was open for 39% -> 0% of each run, Pallas kernels for 0% -> 0%
where the time goes in v1:
time: 55.1 us; the launch traced here: 54.9 us
  Pallas kernels  53.3 us (97%)
  other arithmetic  1.63 us (3%)
    pallas_call x1, Pallas kernels, per_device(): pl.pallas_call(functools.partial(kernel, nrows, nedges), out_shape=jax.Sh...  53.3 us
    convert_element_type x1, other arithmetic, per_device(): return result.astype(F32)  1.63 us

profile of v1, /device:TPU:6, one launch (start us, length us, event | category | flops | bytes accessed | tf_op | source)
XLA Modules:
  0.0 54.9 jit_solution(6833749136183237044)
XLA Ops:
  0.0 53.3 %filter.1 = bf16[32,2048]{1,0:T(8,128)(2,1)} custom-call(bf16[1280,256]{1,0:T(8,128)(2,1)} %feat.1, s32[10,128]{1,0:T(8,128)} %bitcast.3, s32[10,128]{1,0:T(8,128)} %bitcast.4, s32[10,128]{1,0:T(8,128)} %bitcast.5, bf16[3,512]{1,0:T(4,128)(2,1)} %bias.1, bf16[256,512]{1,0:T(8,128)(2,1)} %w_in.1, bf16[256,256]{1,0:T(8,128)(2,1)} %w_out.1, f32[32,2048]{1,0:T(8,128)} %vec.1, ...), custom_call_target="tpu_custom_call" | custom-call | tf_op jit(solution)/shard_map/filter/pallas_call | solution.py:320
  53.3 1.6 %convert_element_type.3 = f32[32,2048]{1,0:T(8,128)} convert(bf16[32,2048]{1,0:T(8,128)(2,1)} %filter.1) | non-fusion elementwise | flops 65536 | bytes 393216 | tf_op jit(solution)/shard_map/convert_element_type | solution.py:363

commit v2 on v1

v2 whole, which is shorter than its diff:
```python
import functools

import jax
import jax.numpy as jnp
from jax import lax
from jax.experimental import pallas as pl
from jax.experimental.pallas import tpu as pltpu
from jax.sharding import PartitionSpec as P

MESH = pl.DeviceIdType.MESH
BF16 = jnp.bfloat16
F32 = jnp.float32

ORB = 16
TILE_ATOMS = 8
BAND = 3
NBAND = 2 * BAND + 1
HID = 256
VEC = 128
STEPS = 4
ATOM_Q = 32
SPILL = 320
E_DEV = 1280
TILE = TILE_ATOMS * ORB
TROWS = ATOM_Q // TILE_ATOMS
OWN = TROWS * TILE
HALO = BAND * TILE
WIDE = OWN + 2 * HALO
LANES = 128
IDROWS = E_DEV // LANES
PAIRS = TROWS // 2
SLOTS_I = 2 * NBAND * TILE_ATOMS
SLOTS = TILE_ATOMS * SLOTS_I
ENDS = 384
PAD = ENDS - SPILL
GROUPS = 2
GROWS = VEC // GROUPS


def kernel(
    nrows, nedges,
    feat, src, dst, cell, bias, w_in, w_out, vec, coef,
    out,
    fown, fends, ids_own, ids_low, ids_high, bias_v, coef_s, win_v, wout_v, wperm, vec_v, vsend,
    slots, cells, onehot_ends, blk, cmat, ht32, ht, tw, tf, res,
    loc_sem, ids_send, ids_recv, feat_send, feat_recv, win_send, win_recv, rim_send, rim_recv,
    halo_send, halo_recv, fin_send, fin_recv,
):
    r = lax.axis_index("rows")
    x = lax.axis_index("edges")
    quarter = r * nedges + x
    ntiles = nrows * nedges * TROWS
    own_vecs = VEC // nedges

    up_x = lax.rem(x + 1, nedges)
    up_r = lax.rem(r + (x + 1) // nedges, nrows)
    down_x = lax.rem(x + nedges - 1, nedges)
    down_r = lax.rem(r + nrows - 1 + (x + nedges - 1) // nedges, nrows)
    up = (up_r, up_x)
    down = (down_r, down_x)

    def remote(source, target, send, recv, device):
        return pltpu.make_async_remote_copy(
            src_ref=source, dst_ref=target, send_sem=send, recv_sem=recv,
            device_id=device, device_id_type=MESH,
        )

    loads = [
        pltpu.make_async_copy(vec, vec_v, loc_sem.at[0]),
        pltpu.make_async_copy(w_out, wout_v, loc_sem.at[1]),
        pltpu.make_async_copy(w_in, win_v, loc_sem.at[2]),
        pltpu.make_async_copy(bias, bias_v, loc_sem.at[3]),
        pltpu.make_async_copy(feat, fown, loc_sem.at[4]),
        pltpu.make_async_copy(src, ids_own.at[0], loc_sem.at[5]),
        pltpu.make_async_copy(dst, ids_own.at[1], loc_sem.at[6]),
        pltpu.make_async_copy(cell, ids_own.at[2], loc_sem.at[7]),
        pltpu.make_async_copy(coef, coef_s, loc_sem.at[8]),
    ]
    for load in loads:
        load.start()

    barrier = pltpu.get_barrier_semaphore()
    after_r = lax.rem(r + 1, nrows)
    before_r = lax.rem(r + nrows - 1, nrows)

    def greet(device):
        pl.semaphore_signal(barrier, inc=1, device_id=device, device_id_type=MESH)

    for device in [up, down] + [(r, lax.rem(x + off, nedges)) for off in range(1, nedges)]:
        greet(device)

    @pl.when(x == 0)
    def _():
        for n in range(nedges):
            greet((before_r, n))

    @pl.when(x == nedges - 1)
    def _():
        for n in range(nedges):
            greet((after_r, n))

    loads[0].wait()
    vsend[...] = vec_v[...].astype(BF16)
    own_cols = pl.ds(pl.multiple_of(x * OWN, OWN), OWN)
    own_rows = pl.ds(pl.multiple_of(x * own_vecs, own_vecs), own_vecs)
    fends[0:PAD, :] = jnp.zeros((PAD, HID), BF16)
    fends[2 * ENDS - PAD : 2 * ENDS, :] = jnp.zeros((PAD, HID), BF16)

    pl.semaphore_wait(barrier, nedges + 3)

    id_copies = []
    for n, ref in enumerate((src, dst, cell)):
        id_copies.append(remote(ref, ids_low.at[n], ids_send.at[0, n], ids_recv.at[0, n], up))
        id_copies.append(remote(ref, ids_high.at[n], ids_send.at[1, n], ids_recv.at[1, n], down))
    feat_copies = [
        remote(feat.at[E_DEV - SPILL : E_DEV], fends.at[PAD:ENDS], feat_send.at[0], feat_recv.at[0], up),
        remote(feat.at[0:SPILL], fends.at[ENDS : ENDS + SPILL], feat_send.at[1], feat_recv.at[1], down),
    ]
    for copy in id_copies + feat_copies:
        copy.start()
    loads[1].wait()
    k_id = lax.broadcasted_iota(jnp.int32, (HID, HID), 0)
    n_id = lax.broadcasted_iota(jnp.int32, (HID, HID), 1)
    swap = jnp.logical_and(n_id // ORB == k_id % ORB, n_id % ORB == k_id // ORB)
    perm = jnp.where(swap, 1.0, 0.0).astype(BF16)
    wperm[...] = jnp.dot(wout_v[...], perm, preferred_element_type=F32).astype(BF16)
    for load in loads[2:]:
        load.wait()
    half = jnp.where(lax.broadcasted_iota(jnp.int32, (1, 2 * HID), 1) < HID, 0.5, 1.0)
    win_v[...] = (win_v[...].astype(F32) * half).astype(BF16)
    bias_of = [bias_v[n : n + 1, :].astype(F32) * half for n in range(3)]

    def spread_cells(row, at):
        cells[at : at + LANES, :] = jnp.broadcast_to(row.astype(F32), (LANES, LANES)).T

    def pair_net(features, at):
        rows = slice(at, at + 2 * LANES)
        kind = cells[rows, :]
        second, third = kind > 0.5, kind > 1.5
        pre = jnp.dot(features, win_v[...], preferred_element_type=F32)
        parts = []
        for c in range(0, 2 * HID, LANES):
            b0, b1, b2 = [b[:, c : c + LANES] for b in bias_of]
            parts.append(pre[:, c : c + LANES] + jnp.where(third, b2, jnp.where(second, b1, b0)))
        hidden = []
        for n in range(HID // LANES):
            gate = parts[n]
            hidden.append(((gate + gate * jnp.tanh(gate)) * parts[n + HID // LANES]).astype(BF16))
        hidden = jnp.concatenate(hidden, axis=1)
        blk[rows, :] = jnp.dot(hidden, wperm[...], preferred_element_type=F32).astype(BF16)

    def slot_ids(ids):
        source = ids[0]
        goal = ids[1]
        local = source % ATOM_Q
        shift = goal // TILE_ATOMS - source // TILE_ATOMS + BAND
        shift = jnp.where(shift < 0, shift + ntiles, shift)
        shift = jnp.where(shift >= ntiles, shift - ntiles, shift)
        tile = local // TILE_ATOMS
        slot = (
            tile // 2 * SLOTS
            + (local % TILE_ATOMS) * SLOTS_I
            + (tile % 2 * NBAND + shift) * TILE_ATOMS
            + goal % TILE_ATOMS
        )
        return jnp.where(source // ATOM_Q == quarter, slot, -1)

    for c in range(IDROWS // 2):
        at = 2 * c * LANES
        for n in range(2):
            spread_cells(ids_own[2, 2 * c + n : 2 * c + n + 1, :], at + n * LANES)
        pair_net(fown[at : at + 2 * LANES, :], at)

    windows = []
    for n in range(nedges):
        first = max(n * OWN - HALO, 0)
        last = min((n + 1) * OWN + HALO, nedges * OWN)
        at = first - (n * OWN - HALO)
        windows.append((first, last, at))

    def window(n, source):
        first, last, at = windows[n]
        rows = pl.ds(pl.multiple_of(source * own_vecs, own_vecs), own_vecs)
        return remote(
            vsend.at[:, first:last], tw.at[0, rows, at : at + last - first],
            win_send.at[n], win_recv.at[source], (r, n),
        )

    for n in range(nedges):

        @pl.when(x != n)
        def _(n=n):
            window(n, x).start()

        @pl.when(x == n)
        def _(n=n):
            first, last, at = windows[n]
            tw[0, own_rows, at : at + last - first] = vsend[:, first:last]

    def rim(side, source):
        rows = pl.ds(pl.multiple_of(source * own_vecs, own_vecs), own_vecs)
        if side == 0:
            source_cols, cols, device = slice(nedges * OWN - HALO, nedges * OWN), slice(0, HALO), (after_r, 0)
        else:
            source_cols, cols, device = slice(0, HALO), slice(HALO + OWN, WIDE), (before_r, nedges - 1)
        return remote(
            vsend.at[:, source_cols], tw.at[0, rows, cols],
            rim_send.at[side], rim_recv.at[side, source], device,
        )

    own_rims = [rim(side, x) for side in range(2)]
    for copy in own_rims:
        copy.start()

    own_slots = slot_ids(ids_own)
    for c in range(IDROWS):
        slots[:, c * LANES : (c + 1) * LANES] = own_slots[c : c + 1, :]

    place = lax.broadcasted_iota(jnp.int32, (SLOTS, 1), 0)

    @pl.loop(0, PAIRS)
    def _(pair):
        row = slots[:, 0:E_DEV] - pair * SLOTS
        onehot = jnp.where(row == place, 1.0, 0.0).astype(BF16)
        own = jnp.dot(onehot, blk[0:E_DEV, :], preferred_element_type=F32)
        cmat[pair] = own.astype(BF16)

    def halo(step, group, rows):
        return [
            remote(
                tw.at[step, rows, HALO + OWN - HALO : HALO + OWN], tw.at[step, rows, 0:HALO],
                halo_send.at[step, 0, group], halo_recv.at[step, 0, group], up,
            ),
            remote(
                tw.at[step, rows, HALO : 2 * HALO], tw.at[step, rows, HALO + OWN : WIDE],
                halo_send.at[step, 1, group], halo_recv.at[step, 1, group], down,
            ),
        ]

    group_rows = [slice(g * GROWS, (g + 1) * GROWS) for g in range(GROUPS)]
    halos = {}

    for copy in id_copies:
        copy.wait_recv()
    low_slots = slot_ids(ids_low)
    high_slots = slot_ids(ids_high)
    nends = ENDS // LANES
    for c in range(nends):
        low_row = slice(IDROWS - nends + c, IDROWS - nends + c + 1)
        high_row = slice(c, c + 1)
        at = E_DEV + c * LANES
        slots[:, at : at + LANES] = low_slots[low_row, :]
        spread_cells(ids_low[2, low_row, :], at)
        at = at + ENDS
        slots[:, at : at + LANES] = high_slots[high_row, :]
        spread_cells(ids_high[2, high_row, :], at)

    @pl.loop(0, PAIRS)
    def _(pair):
        row = slots[:, E_DEV : E_DEV + 2 * ENDS] - pair * SLOTS
        onehot_ends[pair] = jnp.where(row == place, 1.0, 0.0).astype(BF16)

    for copy in feat_copies:
        copy.wait_recv()
    for c in range(nends):
        at = 2 * c * LANES
        pair_net(fends[at : at + 2 * LANES, :], E_DEV + at)

    lane = lax.broadcasted_iota(jnp.int32, (16, LANES), 1)
    upper = [(lane & (ORB << bit)) != 0 for bit in range(3)]
    for pair in range(PAIRS):
        ends = jnp.dot(
            onehot_ends[pair], blk[E_DEV : E_DEV + 2 * ENDS, :], preferred_element_type=F32
        )
        placed = cmat[pair] + ends.astype(BF16)
        for k in range(NBAND):
            for side in range(2):
                cols = slice(side * LANES, (side + 1) * LANES)
                parts = []
                for i in range(TILE_ATOMS):
                    at = i * SLOTS_I + 16 * k
                    parts.append(placed[at : at + 16, cols])
                for bit in range(3):
                    width = ORB << bit
                    for n in range(8):
                        if n & (1 << bit):
                            continue
                        m = n | (1 << bit)
                        first = jnp.where(upper[bit], pltpu.roll(parts[m], width, 1), parts[n])
                        second = jnp.where(upper[bit], parts[m], pltpu.roll(parts[n], LANES - width, 1))
                        parts[n], parts[m] = first, second
                for n in range(8):
                    both = parts[n].astype(F32)
                    for s in range(2):
                        start = (pair * 2 * NBAND + 2 * k + s) * TILE + side * 8 + n
                        ht32[pl.ds(start, 8, stride=ORB), :] = both[8 * s : 8 * s + 8, :]
        ht[pair, NBAND * TILE : (NBAND + 1) * TILE, 0:TILE] = jnp.zeros((TILE, TILE), BF16)
        ht[pair, 0:TILE, TILE : 2 * TILE] = jnp.zeros((TILE, TILE), BF16)
        for a in range(2):
            t = 2 * pair + a
            piece = ht32[t * NBAND * TILE : (t + 1) * NBAND * TILE, :].astype(BF16)
            ht[pair, a * TILE : (a + NBAND) * TILE, a * TILE : (a + 1) * TILE] = piece

    for n in range(nedges):

        @pl.when(x == n)
        def _(n=n):
            for source in range(nedges):
                if source != n:
                    window(n, source).wait_recv()
                if n == 0:
                    rim(0, source).wait_recv()
                if n == nedges - 1:
                    rim(1, source).wait_recv()

    finals = []
    for step in range(1, STEPS + 1):
        for g in range(GROUPS):
            rows = group_rows[g]
            if step > 1:
                for copy in halos[step - 1, g]:
                    copy.wait_recv()
            for pair in range(PAIRS):
                cols = slice(pair * 2 * TILE, (pair + 1) * 2 * TILE)
                wide = slice(pair * 2 * TILE, pair * 2 * TILE + (NBAND + 1) * TILE)
                product = jnp.dot(tw[step - 1, rows, wide], ht[pair], preferred_element_type=F32)
                mid = slice(HALO + pair * 2 * TILE, HALO + (pair + 1) * 2 * TILE)
                if step == 1:
                    new = product
                    total = coef_s[0] * tw[0, rows, mid].astype(F32) + coef_s[1] * new
                else:
                    if step == 2:
                        older = tw[0, rows, mid].astype(F32)
                    else:
                        older = tf[step - 3, rows, cols]
                    new = 2.0 * product - older
                    total = res[rows, cols] + coef_s[step] * new
                if step < STEPS:
                    tw[step, rows, mid] = new.astype(BF16)
                if step < STEPS - 1:
                    tf[step - 1, rows, cols] = new
                if step < STEPS:
                    res[rows, cols] = total
                else:
                    fsend = tw.at[STEPS]
                    fsend[rows, cols] = total.astype(BF16)
            if step < STEPS:
                halos[step, g] = halo(step, g, rows)
                for copy in halos[step, g]:
                    copy.start()
            else:
                for owner in range(g * GROWS // own_vecs, (g + 1) * GROWS // own_vecs):
                    vecs = slice(owner * own_vecs, (owner + 1) * own_vecs)
                    copy = remote(
                        tw.at[STEPS, vecs, 0:OWN], out.at[:, own_cols],
                        fin_send.at[owner], fin_recv.at[x], (r, owner),
                    )
                    finals.append(copy)

                    @pl.when(x != owner)
                    def _(copy=copy):
                        copy.start()

                    @pl.when(x == owner)
                    def _(vecs=vecs):
                        out[:, own_cols] = tw[STEPS, vecs, 0:OWN]

    for copy in id_copies + feat_copies + own_rims:
        copy.wait_send()
    for n in range(nedges):

        @pl.when(x != n)
        def _(n=n):
            window(n, x).wait_send()
    for pair in halos.values():
        for copy in pair:
            copy.wait_send()
    for owner in range(nedges):

        @pl.when(x != owner)
        def _(owner=owner):
            finals[owner].wait_send()
            remote(
                tw.at[STEPS, 0:own_vecs, 0:OWN], out.at[:, owner * OWN : (owner + 1) * OWN],
                fin_send.at[owner], fin_recv.at[owner], (r, owner),
            ).wait_recv()


def per_device(nrows, nedges, features, edge_src, edge_dst, edge_cell, cell_bias, w_in, w_out, vectors, cheb_coef):
    ids = [a.reshape(IDROWS, LANES) for a in (edge_src, edge_dst, edge_cell)]
    own_vecs = VEC // nedges
    dma = pltpu.SemaphoreType.DMA
    anywhere = pl.BlockSpec(memory_space=pl.ANY)
    result = pl.pallas_call(
        functools.partial(kernel, nrows, nedges),
        out_shape=jax.ShapeDtypeStruct(vectors.shape, BF16),
        in_specs=[anywhere] * 9,
        out_specs=pl.BlockSpec(memory_space=pltpu.VMEM),
        scratch_shapes=[
            pltpu.VMEM((E_DEV, HID), BF16),
            pltpu.VMEM((2 * ENDS, HID), BF16),
            pltpu.VMEM((3, IDROWS, LANES), jnp.int32),
            pltpu.VMEM((3, IDROWS, LANES), jnp.int32),
            pltpu.VMEM((3, IDROWS, LANES), jnp.int32),
            pltpu.VMEM((3, 2 * HID), BF16),
            pltpu.SMEM((STEPS + 1,), F32),
            pltpu.VMEM((HID, 2 * HID), BF16),
            pltpu.VMEM((HID, HID), BF16),
            pltpu.VMEM((HID, HID), BF16),
            pltpu.VMEM(vectors.shape, F32),
            pltpu.VMEM(vectors.shape, BF16),
            pltpu.VMEM((1, E_DEV + 2 * ENDS), jnp.int32),
            pltpu.VMEM((E_DEV + 2 * ENDS, LANES), F32),
            pltpu.VMEM((PAIRS, SLOTS, 2 * ENDS), BF16),
            pltpu.VMEM((E_DEV + 2 * ENDS, HID), BF16),
            pltpu.VMEM((PAIRS, SLOTS, HID), BF16),
            pltpu.VMEM((TROWS * NBAND * TILE, TILE), F32),
            pltpu.VMEM((PAIRS, (NBAND + 1) * TILE, 2 * TILE), BF16),
            pltpu.VMEM((STEPS + 1, VEC, WIDE), BF16),
            pltpu.VMEM((STEPS - 2, VEC, OWN), F32),
            pltpu.VMEM((VEC, OWN), F32),
            dma((9,)),
            dma((2, 3)),
            dma((2, 3)),
            dma((2,)),
            dma((2,)),
            dma((nedges,)),
            dma((nedges,)),
            dma((2,)),
            dma((2, nedges)),
            dma((STEPS, 2, GROUPS)),
            dma((STEPS, 2, GROUPS)),
            dma((nedges,)),
            dma((nedges,)),
        ],
        compiler_params=pltpu.CompilerParams(
            collective_id=0, has_side_effects=True
        ),
        name="filter",
    )(features, *ids, cell_bias, w_in, w_out, vectors, cheb_coef)
    return result.astype(F32)


def solution(mesh):
    nrows, nedges = mesh.shape["rows"], mesh.shape["edges"]
    placed = (
        P(("rows", "edges"), None),
        P(("rows", "edges")),
        P(("rows", "edges")),
        P(("rows", "edges")),
        P(),
        P(),
        P(),
        P("edges", "rows"),
        P(),
    )
    return jax.shard_map(
        functools.partial(per_device, nrows, nedges),
        mesh=mesh,
        in_specs=placed,
        out_specs=P("edges", "rows"),
        check_vma=False,
    )
```

time: 55.1 us -> 47.8 us (0.87)
  Pallas kernels: 53.3 us -> 46 us
    pallas_call x1, Pallas kernels: 53.3 us -> 46 us  [per_device(): pl.pallas_call(functools.partial(kernel, nrows, nedges), out_shape=jax.Sh...]
where the time goes in v2:
time: 47.8 us; the launch traced here: 47.7 us
  Pallas kernels  46 us (96%)
  other arithmetic  1.63 us (3%)
    pallas_call x1, Pallas kernels, per_device(): pl.pallas_call(functools.partial(kernel, nrows, nedges), out_shape=jax.Sh...  46 us
    convert_element_type x1, other arithmetic, per_device(): return result.astype(F32)  1.63 us

profile of v2, /device:TPU:6, one launch (start us, length us, event | category | flops | bytes accessed | tf_op | source)
XLA Modules:
  0.0 47.7 jit_solution(3748806879165677285)
XLA Ops:
  0.0 46.0 %filter.1 = bf16[32,2048]{1,0:T(8,128)(2,1)} custom-call(bf16[1280,256]{1,0:T(8,128)(2,1)} %feat.1, s32[10,128]{1,0:T(8,128)} %bitcast.3, s32[10,128]{1,0:T(8,128)} %bitcast.4, s32[10,128]{1,0:T(8,128)} %bitcast.5, bf16[3,512]{1,0:T(4,128)(2,1)} %bias.1, bf16[256,512]{1,0:T(8,128)(2,1)} %w_in.1, bf16[256,256]{1,0:T(8,128)(2,1)} %w_out.1, f32[32,2048]{1,0:T(8,128)} %vec.1, ...), custom_call_target="tpu_custom_call" | custom-call | tf_op jit(solution)/shard_map/filter/pallas_call | solution.py:394
  46.1 1.6 %convert_element_type.3 = f32[32,2048]{1,0:T(8,128)} convert(bf16[32,2048]{1,0:T(8,128)(2,1)} %filter.1) | non-fusion elementwise | flops 65536 | bytes 393216 | tf_op jit(solution)/shard_map/convert_element_type | solution.py:441

commit v3 on v2

--- a/solution.py
+++ b/solution.py
@@ -42,7 +42,7 @@
     feat, src, dst, cell, bias, w_in, w_out, vec, coef,
     out,
     fown, fends, ids_own, ids_low, ids_high, bias_v, coef_s, win_v, wout_v, wperm, vec_v, vsend,
-    slots, cells, onehot_ends, blk, cmat, ht32, ht, tw, tf, res,
+    slots, cells, onehot_ends, hid, blk, cmat, ht32, ht, tw, tf, res,
     loc_sem, ids_send, ids_recv, feat_send, feat_recv, win_send, win_recv, rim_send, rim_recv,
     halo_send, halo_recv, fin_send, fin_recv,
 ):
@@ -99,25 +99,6 @@
         for n in range(nedges):
             greet((after_r, n))
 
-    loads[0].wait()
-    vsend[...] = vec_v[...].astype(BF16)
-    own_cols = pl.ds(pl.multiple_of(x * OWN, OWN), OWN)
-    own_rows = pl.ds(pl.multiple_of(x * own_vecs, own_vecs), own_vecs)
-    fends[0:PAD, :] = jnp.zeros((PAD, HID), BF16)
-    fends[2 * ENDS - PAD : 2 * ENDS, :] = jnp.zeros((PAD, HID), BF16)
-
-    pl.semaphore_wait(barrier, nedges + 3)
-
-    id_copies = []
-    for n, ref in enumerate((src, dst, cell)):
-        id_copies.append(remote(ref, ids_low.at[n], ids_send.at[0, n], ids_recv.at[0, n], up))
-        id_copies.append(remote(ref, ids_high.at[n], ids_send.at[1, n], ids_recv.at[1, n], down))
-    feat_copies = [
-        remote(feat.at[E_DEV - SPILL : E_DEV], fends.at[PAD:ENDS], feat_send.at[0], feat_recv.at[0], up),
-        remote(feat.at[0:SPILL], fends.at[ENDS : ENDS + SPILL], feat_send.at[1], feat_recv.at[1], down),
-    ]
-    for copy in id_copies + feat_copies:
-        copy.start()
     loads[1].wait()
     k_id = lax.broadcasted_iota(jnp.int32, (HID, HID), 0)
     n_id = lax.broadcasted_iota(jnp.int32, (HID, HID), 1)
@@ -130,24 +111,25 @@
     win_v[...] = (win_v[...].astype(F32) * half).astype(BF16)
     bias_of = [bias_v[n : n + 1, :].astype(F32) * half for n in range(3)]
 
-    def spread_cells(row, at):
-        cells[at : at + LANES, :] = jnp.broadcast_to(row.astype(F32), (LANES, LANES)).T
-
-    def pair_net(features, at):
-        rows = slice(at, at + 2 * LANES)
-        kind = cells[rows, :]
-        second, third = kind > 0.5, kind > 1.5
-        pre = jnp.dot(features, win_v[...], preferred_element_type=F32)
-        parts = []
-        for c in range(0, 2 * HID, LANES):
-            b0, b1, b2 = [b[:, c : c + LANES] for b in bias_of]
-            parts.append(pre[:, c : c + LANES] + jnp.where(third, b2, jnp.where(second, b1, b0)))
-        hidden = []
-        for n in range(HID // LANES):
-            gate = parts[n]
-            hidden.append(((gate + gate * jnp.tanh(gate)) * parts[n + HID // LANES]).astype(BF16))
-        hidden = jnp.concatenate(hidden, axis=1)
-        blk[rows, :] = jnp.dot(hidden, wperm[...], preferred_element_type=F32).astype(BF16)
+    def pair_net(at, count):
+        for n in range(at, at + count, LANES):
+            row = ids_own[2, n // LANES : n // LANES + 1, :]
+            cells[n : n + LANES, :] = jnp.broadcast_to(row.astype(F32), (LANES, LANES)).T
+        for first in range(at, at + count, 128):
+            rows = slice(first, first + 128)
+            kind = cells[rows, :]
+            second, third = kind > 0.5, kind > 1.5
+            pre = jnp.dot(fown[rows, :], win_v[...], preferred_element_type=F32)
+            parts = []
+            for c in range(0, 2 * HID, LANES):
+                b0, b1, b2 = [b[:, c : c + LANES] for b in bias_of]
+                parts.append(pre[:, c : c + LANES] + jnp.where(third, b2, jnp.where(second, b1, b0)))
+            for n in range(HID // LANES):
+                gate = parts[n]
+                value = (gate + gate * jnp.tanh(gate)) * parts[n + HID // LANES]
+                hid[rows, n * LANES : (n + 1) * LANES] = value.astype(BF16)
+        rows = slice(at, at + count)
+        blk[rows, :] = jnp.dot(hid[rows, :], wperm[...], preferred_element_type=F32).astype(BF16)
 
     def slot_ids(ids):
         source = ids[0]
@@ -165,11 +147,30 @@
         )
         return jnp.where(source // ATOM_Q == quarter, slot, -1)
 
-    for c in range(IDROWS // 2):
-        at = 2 * c * LANES
-        for n in range(2):
-            spread_cells(ids_own[2, 2 * c + n : 2 * c + n + 1, :], at + n * LANES)
-        pair_net(fown[at : at + 2 * LANES, :], at)
+    ends_rows = (slice(0, ENDS), slice(E_DEV - ENDS, E_DEV))
+    for rows in ends_rows:
+        pair_net(rows.start, ENDS)
+
+    loads[0].wait()
+    vsend[...] = vec_v[...].astype(BF16)
+    own_cols = pl.ds(pl.multiple_of(x * OWN, OWN), OWN)
+    own_rows = pl.ds(pl.multiple_of(x * own_vecs, own_vecs), own_vecs)
+    fends[0:PAD, :] = jnp.zeros((PAD, HID), BF16)
+    fends[2 * ENDS - PAD : 2 * ENDS, :] = jnp.zeros((PAD, HID), BF16)
+
+    pl.semaphore_wait(barrier, nedges + 3)
+
+    id_copies = []
+    for n, ref in enumerate((src, dst)):
+        id_copies.append(remote(ref, ids_low.at[n], ids_send.at[0, n], ids_recv.at[0, n], up))
+        id_copies.append(remote(ref, ids_high.at[n], ids_send.at[1, n], ids_recv.at[1, n], down))
+    blk_copies = [
+        remote(blk.at[E_DEV - SPILL : E_DEV], fends.at[PAD:ENDS], feat_send.at[0], feat_recv.at[0], up),
+        remote(blk.at[0:SPILL], fends.at[ENDS : ENDS + SPILL], feat_send.at[1], feat_recv.at[1], down),
+    ]
+    for copy in id_copies + blk_copies:
+        copy.start()
+    pair_net(ENDS, E_DEV - 2 * ENDS)
 
     windows = []
     for n in range(nedges):
@@ -185,17 +186,6 @@
             vsend.at[:, first:last], tw.at[0, rows, at : at + last - first],
             win_send.at[n], win_recv.at[source], (r, n),
         )
-
-    for n in range(nedges):
-
-        @pl.when(x != n)
-        def _(n=n):
-            window(n, x).start()
-
-        @pl.when(x == n)
-        def _(n=n):
-            first, last, at = windows[n]
-            tw[0, own_rows, at : at + last - first] = vsend[:, first:last]
 
     def rim(side, source):
         rows = pl.ds(pl.multiple_of(source * own_vecs, own_vecs), own_vecs)
@@ -208,22 +198,35 @@
             rim_send.at[side], rim_recv.at[side, source], device,
         )
 
-    own_rims = [rim(side, x) for side in range(2)]
-    for copy in own_rims:
-        copy.start()
-
     own_slots = slot_ids(ids_own)
     for c in range(IDROWS):
         slots[:, c * LANES : (c + 1) * LANES] = own_slots[c : c + 1, :]
 
     place = lax.broadcasted_iota(jnp.int32, (SLOTS, 1), 0)
 
-    @pl.loop(0, PAIRS)
-    def _(pair):
+    def place_own(pair):
         row = slots[:, 0:E_DEV] - pair * SLOTS
         onehot = jnp.where(row == place, 1.0, 0.0).astype(BF16)
         own = jnp.dot(onehot, blk[0:E_DEV, :], preferred_element_type=F32)
         cmat[pair] = own.astype(BF16)
+
+    place_own(0)
+    for n in range(nedges):
+
+        @pl.when(x != n)
+        def _(n=n):
+            window(n, x).start()
+
+        @pl.when(x == n)
+        def _(n=n):
+            first, last, at = windows[n]
+            tw[0, own_rows, at : at + last - first] = vsend[:, first:last]
+
+    own_rims = [rim(side, x) for side in range(2)]
+    for copy in own_rims:
+        copy.start()
+
+    place_own(1)
 
     def halo(step, group, rows):
         return [
@@ -250,27 +253,22 @@
         high_row = slice(c, c + 1)
         at = E_DEV + c * LANES
         slots[:, at : at + LANES] = low_slots[low_row, :]
-        spread_cells(ids_low[2, low_row, :], at)
         at = at + ENDS
         slots[:, at : at + LANES] = high_slots[high_row, :]
-        spread_cells(ids_high[2, high_row, :], at)
 
     @pl.loop(0, PAIRS)
     def _(pair):
         row = slots[:, E_DEV : E_DEV + 2 * ENDS] - pair * SLOTS
         onehot_ends[pair] = jnp.where(row == place, 1.0, 0.0).astype(BF16)
 
-    for copy in feat_copies:
+    for copy in blk_copies:
         copy.wait_recv()
-    for c in range(nends):
-        at = 2 * c * LANES
-        pair_net(fends[at : at + 2 * LANES, :], E_DEV + at)
 
     lane = lax.broadcasted_iota(jnp.int32, (16, LANES), 1)
     upper = [(lane & (ORB << bit)) != 0 for bit in range(3)]
     for pair in range(PAIRS):
         ends = jnp.dot(
-            onehot_ends[pair], blk[E_DEV : E_DEV + 2 * ENDS, :], preferred_element_type=F32
+            onehot_ends[pair], fends[...], preferred_element_type=F32
         )
         placed = cmat[pair] + ends.astype(BF16)
         for k in range(NBAND):
@@ -301,23 +299,26 @@
             piece = ht32[t * NBAND * TILE : (t + 1) * NBAND * TILE, :].astype(BF16)
             ht[pair, a * TILE : (a + NBAND) * TILE, a * TILE : (a + 1) * TILE] = piece
 
-    for n in range(nedges):
-
-        @pl.when(x == n)
-        def _(n=n):
-            for source in range(nedges):
-                if source != n:
-                    window(n, source).wait_recv()
-                if n == 0:
-                    rim(0, source).wait_recv()
-                if n == nedges - 1:
-                    rim(1, source).wait_recv()
+    def wait_windows(sources):
+        for n in range(nedges):
+
+            @pl.when(x == n)
+            def _(n=n):
+                for source in sources:
+                    if source != n:
+                        window(n, source).wait_recv()
+                    if n == 0:
+                        rim(0, source).wait_recv()
+                    if n == nedges - 1:
+                        rim(1, source).wait_recv()
 
     finals = []
     for step in range(1, STEPS + 1):
         for g in range(GROUPS):
             rows = group_rows[g]
-            if step > 1:
+            if step == 1:
+                wait_windows(range(g * GROWS // own_vecs, (g + 1) * GROWS // own_vecs))
+            else:
                 for copy in halos[step - 1, g]:
                     copy.wait_recv()
             for pair in range(PAIRS):
@@ -363,9 +364,9 @@
 
                     @pl.when(x == owner)
                     def _(vecs=vecs):
-                        out[:, own_cols] = tw[STEPS, vecs, 0:OWN]
-
-    for copy in id_copies + feat_copies + own_rims:
+                        pltpu.make_async_copy(tw.at[STEPS, vecs, 0:OWN], out.at[:, own_cols], loc_sem.at[9]).start()
+
+    for copy in id_copies + blk_copies + own_rims:
         copy.wait_send()
     for n in range(nedges):
 
@@ -375,6 +376,7 @@
     for pair in halos.values():
         for copy in pair:
             copy.wait_send()
+    pltpu.make_async_copy(tw.at[STEPS, 0:own_vecs, 0:OWN], out.at[:, own_cols], loc_sem.at[9]).wait()
     for owner in range(nedges):
 
         @pl.when(x != owner)
@@ -395,13 +397,13 @@
         functools.partial(kernel, nrows, nedges),
         out_shape=jax.ShapeDtypeStruct(vectors.shape, BF16),
         in_specs=[anywhere] * 9,
-        out_specs=pl.BlockSpec(memory_space=pltpu.VMEM),
+        out_specs=anywhere,
         scratch_shapes=[
             pltpu.VMEM((E_DEV, HID), BF16),
             pltpu.VMEM((2 * ENDS, HID), BF16),
             pltpu.VMEM((3, IDROWS, LANES), jnp.int32),
-            pltpu.VMEM((3, IDROWS, LANES), jnp.int32),
-            pltpu.VMEM((3, IDROWS, LANES), jnp.int32),
+            pltpu.VMEM((2, IDROWS, LANES), jnp.int32),
+            pltpu.VMEM((2, IDROWS, LANES), jnp.int32),
             pltpu.VMEM((3, 2 * HID), BF16),
             pltpu.SMEM((STEPS + 1,), F32),
             pltpu.VMEM((HID, 2 * HID), BF16),
@@ -410,18 +412,19 @@
             pltpu.VMEM(vectors.shape, F32),
             pltpu.VMEM(vectors.shape, BF16),
             pltpu.VMEM((1, E_DEV + 2 * ENDS), jnp.int32),
-            pltpu.VMEM((E_DEV + 2 * ENDS, LANES), F32),
+            pltpu.VMEM((E_DEV, LANES), F32),
             pltpu.VMEM((PAIRS, SLOTS, 2 * ENDS), BF16),
-            pltpu.VMEM((E_DEV + 2 * ENDS, HID), BF16),
+            pltpu.VMEM((E_DEV, HID), BF16),
+            pltpu.VMEM((E_DEV, HID), BF16),
             pltpu.VMEM((PAIRS, SLOTS, HID), BF16),
             pltpu.VMEM((TROWS * NBAND * TILE, TILE), F32),
             pltpu.VMEM((PAIRS, (NBAND + 1) * TILE, 2 * TILE), BF16),
             pltpu.VMEM((STEPS + 1, VEC, WIDE), BF16),
             pltpu.VMEM((STEPS - 2, VEC, OWN), F32),
             pltpu.VMEM((VEC, OWN), F32),
-            dma((9,)),
-            dma((2, 3)),
-            dma((2, 3)),
+            dma((10,)),
+            dma((2, 2)),
+            dma((2, 2)),
             dma((2,)),
             dma((2,)),
             dma((nedges,)),

time: 47.8 us -> 46.7 us (0.977)
  Pallas kernels: 46 us -> 44.9 us
    pallas_call x1, Pallas kernels: 46 us -> 44.9 us  [per_device(): pl.pallas_call(functools.partial(kernel, nrows, nedges), out_shape=jax.Sh...]
where the time goes in v3:
time: 46.7 us; the launch traced here: 46.5 us
  Pallas kernels  44.9 us (96%)
  other arithmetic  1.63 us (3%)
    pallas_call x1, Pallas kernels, per_device(): pl.pallas_call(functools.partial(kernel, nrows, nedges), out_shape=jax.Sh...  44.9 us
    convert_element_type x1, other arithmetic, per_device(): return result.astype(F32)  1.63 us

profile of v3, /device:TPU:6, one launch (start us, length us, event | category | flops | bytes accessed | tf_op | source)
XLA Modules:
  0.0 46.5 jit_solution(2133797305999732200)
XLA Ops:
  0.0 44.9 %filter.1 = bf16[32,2048]{1,0:T(8,128)(2,1)} custom-call(bf16[1280,256]{1,0:T(8,128)(2,1)} %feat.1, s32[10,128]{1,0:T(8,128)} %bitcast.3, s32[10,128]{1,0:T(8,128)} %bitcast.4, s32[10,128]{1,0:T(8,128)} %bitcast.5, bf16[3,512]{1,0:T(4,128)(2,1)} %bias.1, bf16[256,512]{1,0:T(8,128)(2,1)} %w_in.1, bf16[256,256]{1,0:T(8,128)(2,1)} %w_out.1, f32[32,2048]{1,0:T(8,128)} %vec.1, ...), custom_call_target="tpu_custom_call" | custom-call | tf_op jit(solution)/shard_map/filter/pallas_call | solution.py:396
  44.9 1.6 %convert_element_type.3 = f32[32,2048]{1,0:T(8,128)} convert(bf16[32,2048]{1,0:T(8,128)(2,1)} %filter.1) | non-fusion elementwise | flops 65536 | bytes 393216 | tf_op jit(solution)/shard_map/convert_element_type | solution.py:444

commit v4 on v3

--- a/solution.py
+++ b/solution.py
@@ -76,9 +76,6 @@
         pltpu.make_async_copy(cell, ids_own.at[2], loc_sem.at[7]),
         pltpu.make_async_copy(coef, coef_s, loc_sem.at[8]),
     ]
-    for load in loads:
-        load.start()
-
     barrier = pltpu.get_barrier_semaphore()
     after_r = lax.rem(r + 1, nrows)
     before_r = lax.rem(r + nrows - 1, nrows)
@@ -98,6 +95,9 @@
     def _():
         for n in range(nedges):
             greet((after_r, n))
+
+    for load in loads:
+        load.start()
 
     loads[1].wait()
     k_id = lax.broadcasted_iota(jnp.int32, (HID, HID), 0)
@@ -264,40 +264,42 @@
     for copy in blk_copies:
         copy.wait_recv()
 
-    lane = lax.broadcasted_iota(jnp.int32, (16, LANES), 1)
-    upper = [(lane & (ORB << bit)) != 0 for bit in range(3)]
+    group = lax.broadcasted_iota(jnp.int32, (16, LANES), 1)
+    odd = [(group & (ORB << bit)) != 0 for bit in range(3)]
     for pair in range(PAIRS):
-        ends = jnp.dot(
-            onehot_ends[pair], fends[...], preferred_element_type=F32
-        )
-        placed = cmat[pair] + ends.astype(BF16)
+        for a in range(2):
+            t = 2 * pair + a
+            free = 0 if a else NBAND * TILE
+            ht[t, free : free + TILE, :] = jnp.zeros((TILE, TILE), BF16)
+        ends = jnp.dot(onehot_ends[pair], fends[...], preferred_element_type=F32)
+        cmat[pair] = cmat[pair] + ends.astype(BF16)
         for k in range(NBAND):
             for side in range(2):
                 cols = slice(side * LANES, (side + 1) * LANES)
                 parts = []
                 for i in range(TILE_ATOMS):
                     at = i * SLOTS_I + 16 * k
-                    parts.append(placed[at : at + 16, cols])
-                for bit in range(3):
-                    width = ORB << bit
-                    for n in range(8):
-                        if n & (1 << bit):
-                            continue
-                        m = n | (1 << bit)
-                        first = jnp.where(upper[bit], pltpu.roll(parts[m], width, 1), parts[n])
-                        second = jnp.where(upper[bit], parts[m], pltpu.roll(parts[n], LANES - width, 1))
-                        parts[n], parts[m] = first, second
-                for n in range(8):
-                    both = parts[n].astype(F32)
+                    part = cmat[pair, at : at + 16, cols]
+                    parts.append(pltpu.roll(part, i * ORB, 1) if i else part)
+                for q in range(8):
+                    level = [parts[(g - q) % 8] for g in range(8)]
+                    for bit in range(3):
+                        level = [
+                            jnp.where(odd[bit], level[n + 1], level[n])
+                            for n in range(0, len(level), 2)
+                        ]
+                    both = pltpu.roll(level[0], LANES - q * ORB, 1) if q else level[0]
+                    both = both.astype(F32)
                     for s in range(2):
-                        start = (pair * 2 * NBAND + 2 * k + s) * TILE + side * 8 + n
-                        ht32[pl.ds(start, 8, stride=ORB), :] = both[8 * s : 8 * s + 8, :]
-        ht[pair, NBAND * TILE : (NBAND + 1) * TILE, 0:TILE] = jnp.zeros((TILE, TILE), BF16)
-        ht[pair, 0:TILE, TILE : 2 * TILE] = jnp.zeros((TILE, TILE), BF16)
-        for a in range(2):
-            t = 2 * pair + a
-            piece = ht32[t * NBAND * TILE : (t + 1) * NBAND * TILE, :].astype(BF16)
-            ht[pair, a * TILE : (a + NBAND) * TILE, a * TILE : (a + 1) * TILE] = piece
+                        start = (pair * 2 * NBAND + 2 * k + s) * TILE + (side * 8 + q) * TILE_ATOMS
+                        ht32[start : start + TILE_ATOMS, :] = both[8 * s : 8 * s + 8, :]
+            for s in range(2):
+                a, d = divmod(2 * k + s, NBAND)
+                for j in range(TILE_ATOMS):
+                    start = (pair * 2 * NBAND + 2 * k + s) * TILE + j
+                    piece = ht32[pl.ds(start, ORB, stride=TILE_ATOMS), :].astype(BF16)
+                    at = (a + d) * TILE + j * ORB
+                    ht[2 * pair + a, at : at + ORB, :] = piece
 
     def wait_windows(sources):
         for n in range(nedges):
@@ -324,7 +326,8 @@
             for pair in range(PAIRS):
                 cols = slice(pair * 2 * TILE, (pair + 1) * 2 * TILE)
                 wide = slice(pair * 2 * TILE, pair * 2 * TILE + (NBAND + 1) * TILE)
-                product = jnp.dot(tw[step - 1, rows, wide], ht[pair], preferred_element_type=F32)
+                band = jnp.concatenate([ht[2 * pair], ht[2 * pair + 1]], axis=1)
+                product = jnp.dot(tw[step - 1, rows, wide], band, preferred_element_type=F32)
                 mid = slice(HALO + pair * 2 * TILE, HALO + (pair + 1) * 2 * TILE)
                 if step == 1:
                     new = product
@@ -418,7 +421,7 @@
             pltpu.VMEM((E_DEV, HID), BF16),
             pltpu.VMEM((PAIRS, SLOTS, HID), BF16),
             pltpu.VMEM((TROWS * NBAND * TILE, TILE), F32),
-            pltpu.VMEM((PAIRS, (NBAND + 1) * TILE, 2 * TILE), BF16),
+            pltpu.VMEM((TROWS, (NBAND + 1) * TILE, TILE), BF16),
             pltpu.VMEM((STEPS + 1, VEC, WIDE), BF16),
             pltpu.VMEM((STEPS - 2, VEC, OWN), F32),
             pltpu.VMEM((VEC, OWN), F32),

time: 46.7 us -> 46.2 us (0.989)
  Pallas kernels: 44.9 us -> 44.4 us
    pallas_call x1, Pallas kernels: 44.9 us -> 44.4 us  [per_device(): pl.pallas_call(functools.partial(kernel, nrows, nedges), out_shape=jax.Sh...]
where the time goes in v4:
time: 46.2 us; the launch traced here: 46 us
  Pallas kernels  44.4 us (96%)
  other arithmetic  1.63 us (4%)
    pallas_call x1, Pallas kernels, per_device(): pl.pallas_call(functools.partial(kernel, nrows, nedges), out_shape=jax.Sh...  44.4 us
    convert_element_type x1, other arithmetic, per_device(): return result.astype(F32)  1.63 us

profile of v4, /device:TPU:6, one launch (start us, length us, event | category | flops | bytes accessed | tf_op | source)
XLA Modules:
  0.0 46.0 jit_solution(16798651349930908207)
XLA Ops:
  0.0 44.4 %filter.1 = bf16[32,2048]{1,0:T(8,128)(2,1)} custom-call(bf16[1280,256]{1,0:T(8,128)(2,1)} %feat.1, s32[10,128]{1,0:T(8,128)} %bitcast.3, s32[10,128]{1,0:T(8,128)} %bitcast.4, s32[10,128]{1,0:T(8,128)} %bitcast.5, bf16[3,512]{1,0:T(4,128)(2,1)} %bias.1, bf16[256,512]{1,0:T(8,128)(2,1)} %w_in.1, bf16[256,256]{1,0:T(8,128)(2,1)} %w_out.1, f32[32,2048]{1,0:T(8,128)} %vec.1, ...), custom_call_target="tpu_custom_call" | custom-call | tf_op jit(solution)/shard_map/filter/pallas_call | solution.py:399
  44.4 1.6 %convert_element_type.3 = f32[32,2048]{1,0:T(8,128)} convert(bf16[32,2048]{1,0:T(8,128)(2,1)} %filter.1) | non-fusion elementwise | flops 65536 | bytes 393216 | tf_op jit(solution)/shard_map/convert_element_type | solution.py:447

commit v5 on v4

--- a/solution.py
+++ b/solution.py
@@ -33,7 +33,7 @@
 SLOTS = TILE_ATOMS * SLOTS_I
 ENDS = 384
 PAD = ENDS - SPILL
-GROUPS = 2
+GROUPS = 4
 GROWS = VEC // GROUPS
 
 
@@ -261,18 +261,18 @@
         row = slots[:, E_DEV : E_DEV + 2 * ENDS] - pair * SLOTS
         onehot_ends[pair] = jnp.where(row == place, 1.0, 0.0).astype(BF16)
 
+    for t in range(TROWS):
+        free = 0 if t % 2 else NBAND * TILE
+        ht[t, free : free + TILE, :] = jnp.zeros((TILE, TILE), BF16)
     for copy in blk_copies:
         copy.wait_recv()
 
     group = lax.broadcasted_iota(jnp.int32, (16, LANES), 1)
     odd = [(group & (ORB << bit)) != 0 for bit in range(3)]
     for pair in range(PAIRS):
-        for a in range(2):
-            t = 2 * pair + a
-            free = 0 if a else NBAND * TILE
-            ht[t, free : free + TILE, :] = jnp.zeros((TILE, TILE), BF16)
         ends = jnp.dot(onehot_ends[pair], fends[...], preferred_element_type=F32)
         cmat[pair] = cmat[pair] + ends.astype(BF16)
+    for pair in range(PAIRS):
         for k in range(NBAND):
             for side in range(2):
                 cols = slice(side * LANES, (side + 1) * LANES)

time: 46.2 us -> 46 us (level)
  no operation moved by 1% of the time
where the time goes in v5:
time: 46 us; the launch traced here: 45.8 us
  Pallas kernels  44.2 us (96%)
  other arithmetic  1.63 us (4%)
    pallas_call x1, Pallas kernels, per_device(): pl.pallas_call(functools.partial(kernel, nrows, nedges), out_shape=jax.Sh...  44.2 us
    convert_element_type x1, other arithmetic, per_device(): return result.astype(F32)  1.63 us

profile of v5, /device:TPU:6, one launch (start us, length us, event | category | flops | bytes accessed | tf_op | source)
XLA Modules:
  0.0 45.8 jit_solution(18327269925165170521)
XLA Ops:
  0.0 44.2 %filter.1 = bf16[32,2048]{1,0:T(8,128)(2,1)} custom-call(bf16[1280,256]{1,0:T(8,128)(2,1)} %feat.1, s32[10,128]{1,0:T(8,128)} %bitcast.3, s32[10,128]{1,0:T(8,128)} %bitcast.4, s32[10,128]{1,0:T(8,128)} %bitcast.5, bf16[3,512]{1,0:T(4,128)(2,1)} %bias.1, bf16[256,512]{1,0:T(8,128)(2,1)} %w_in.1, bf16[256,256]{1,0:T(8,128)(2,1)} %w_out.1, f32[32,2048]{1,0:T(8,128)} %vec.1, ...), custom_call_target="tpu_custom_call" | custom-call | tf_op jit(solution)/shard_map/filter/pallas_call | solution.py:399
  44.2 1.6 %convert_element_type.3 = f32[32,2048]{1,0:T(8,128)} convert(bf16[32,2048]{1,0:T(8,128)(2,1)} %filter.1) | non-fusion elementwise | flops 65536 | bytes 393216 | tf_op jit(solution)/shard_map/convert_element_type | solution.py:447

commit v6 on v5

--- a/solution.py
+++ b/solution.py
@@ -211,20 +211,27 @@
         cmat[pair] = own.astype(BF16)
 
     place_own(0)
+    own_rims = [rim(side, x) for side in range(2)]
+    for copy in own_rims:
+        copy.start()
     for n in range(nedges):
 
-        @pl.when(x != n)
+        @pl.when(lax.rem(x + 2, nedges) == n)
         def _(n=n):
             window(n, x).start()
+
+    for n in range(nedges):
+
+        @pl.when(jnp.logical_and(x != n, lax.rem(x + 2, nedges) != n))
+        def _(n=n):
+            window(n, x).start()
+
+    for n in range(nedges):
 
         @pl.when(x == n)
         def _(n=n):
             first, last, at = windows[n]
             tw[0, own_rows, at : at + last - first] = vsend[:, first:last]
-
-    own_rims = [rim(side, x) for side in range(2)]
-    for copy in own_rims:
-        copy.start()
 
     place_own(1)
 

time: 46 us -> 46 us (level)
  no operation moved by 1% of the time
where the time goes in v6:
time: 46 us; the launch traced here: 45.8 us
  Pallas kernels  44.2 us (96%)
  other arithmetic  1.63 us (4%)
    pallas_call x1, Pallas kernels, per_device(): pl.pallas_call(functools.partial(kernel, nrows, nedges), out_shape=jax.Sh...  44.2 us
    convert_element_type x1, other arithmetic, per_device(): return result.astype(F32)  1.63 us

profile of v6, /device:TPU:6, one launch (start us, length us, event | category | flops | bytes accessed | tf_op | source)
XLA Modules:
  0.0 45.8 jit_solution(17257599312148541812)
XLA Ops:
  0.0 44.2 %filter.1 = bf16[32,2048]{1,0:T(8,128)(2,1)} custom-call(bf16[1280,256]{1,0:T(8,128)(2,1)} %feat.1, s32[10,128]{1,0:T(8,128)} %bitcast.3, s32[10,128]{1,0:T(8,128)} %bitcast.4, s32[10,128]{1,0:T(8,128)} %bitcast.5, bf16[3,512]{1,0:T(4,128)(2,1)} %bias.1, bf16[256,512]{1,0:T(8,128)(2,1)} %w_in.1, bf16[256,256]{1,0:T(8,128)(2,1)} %w_out.1, f32[32,2048]{1,0:T(8,128)} %vec.1, ...), custom_call_target="tpu_custom_call" | custom-call | tf_op jit(solution)/shard_map/filter/pallas_call | solution.py:406
  44.2 1.6 %convert_element_type.3 = f32[32,2048]{1,0:T(8,128)} convert(bf16[32,2048]{1,0:T(8,128)(2,1)} %filter.1) | non-fusion elementwise | flops 65536 | bytes 393216 | tf_op jit(solution)/shard_map/convert_element_type | solution.py:454

commit v7 on v5

--- a/solution.py
+++ b/solution.py
@@ -314,8 +314,24 @@
                     if n == nedges - 1:
                         rim(1, source).wait_recv()
 
+    def drain():
+        for copy in id_copies + blk_copies + own_rims:
+            copy.wait_send()
+        for n in range(nedges):
+
+            @pl.when(x != n)
+            def _(n=n):
+                window(n, x).wait_send()
+
+        for step in range(1, STEPS - 1):
+            for g in range(GROUPS):
+                for copy in halos[step, g]:
+                    copy.wait_send()
+
     finals = []
     for step in range(1, STEPS + 1):
+        if step == STEPS:
+            drain()
         for g in range(GROUPS):
             rows = group_rows[g]
             if step == 1:
@@ -369,15 +385,8 @@
                     def _(vecs=vecs):
                         pltpu.make_async_copy(tw.at[STEPS, vecs, 0:OWN], out.at[:, own_cols], loc_sem.at[9]).start()
 
-    for copy in id_copies + blk_copies + own_rims:
-        copy.wait_send()
-    for n in range(nedges):
-
-        @pl.when(x != n)
-        def _(n=n):
-            window(n, x).wait_send()
-    for pair in halos.values():
-        for copy in pair:
+    for g in range(GROUPS):
+        for copy in halos[STEPS - 1, g]:
             copy.wait_send()
     pltpu.make_async_copy(tw.at[STEPS, 0:own_vecs, 0:OWN], out.at[:, own_cols], loc_sem.at[9]).wait()
     for owner in range(nedges):

time: 46 us -> 46 us (level)
  no operation moved by 1% of the time
where the time goes in v7:
time: 46 us; the launch traced here: 45.8 us
  Pallas kernels  44.2 us (96%)
  other arithmetic  1.63 us (4%)
    pallas_call x1, Pallas kernels, per_device(): pl.pallas_call(functools.partial(kernel, nrows, nedges), out_shape=jax.Sh...  44.2 us
    convert_element_type x1, other arithmetic, per_device(): return result.astype(F32)  1.63 us

profile of v7, /device:TPU:6, one launch (start us, length us, event | category | flops | bytes accessed | tf_op | source)
XLA Modules:
  0.0 45.8 jit_solution(11028028985306161142)
XLA Ops:
  0.0 44.2 %filter.1 = bf16[32,2048]{1,0:T(8,128)(2,1)} custom-call(bf16[1280,256]{1,0:T(8,128)(2,1)} %feat.1, s32[10,128]{1,0:T(8,128)} %bitcast.3, s32[10,128]{1,0:T(8,128)} %bitcast.4, s32[10,128]{1,0:T(8,128)} %bitcast.5, bf16[3,512]{1,0:T(4,128)(2,1)} %bias.1, bf16[256,512]{1,0:T(8,128)(2,1)} %w_in.1, bf16[256,256]{1,0:T(8,128)(2,1)} %w_out.1, f32[32,2048]{1,0:T(8,128)} %vec.1, ...), custom_call_target="tpu_custom_call" | custom-call | tf_op jit(solution)/shard_map/filter/pallas_call | solution.py:408
  44.2 1.6 %convert_element_type.3 = f32[32,2048]{1,0:T(8,128)} convert(bf16[32,2048]{1,0:T(8,128)(2,1)} %filter.1) | non-fusion elementwise | flops 65536 | bytes 393216 | tf_op jit(solution)/shard_map/convert_element_type | solution.py:456
